TPU v7x, 32 devices: a whole 2x2x4 slice. The times are simulated.
32 devices in a mesh: space: 4 (over y, core), energy: 8 (over z, x).
Axes of the slice: x: 2, y: 2, z: 4, core: 2. Of those that a mesh axis runs over, the one named last changes fastest.
Arguments:
- onsite: float32 [2, 8, 64, 64], P(None, 'space'), as said below
- hopping: float32 [2, 8, 64, 64], P(None, 'space'), may hold values from -0.375 to 0.375
- sigma_prior: float32 [2, 8, 8, 64, 64], P(None, 'energy', 'space'), as said below
- screened: float32 [2, 15, 32768], P(None, None, ('space', 'energy')), may hold values from -6 to 6
Outputs:
- sigma_next: float32 [2, 8, 32768], P(None, None, ('space', 'energy'))
Inputs may be any that keep to these rules, and one draw needn't show every extreme that they name: `onsite`: every block is Hermitian: real part symmetric, imaginary part antisymmetric. `sigma_prior`: every block is Hermitian: real part symmetric, imaginary part antisymmetric.
All inputs are finite; a program needn't handle non-finite values.
Results may differ from a plain program's by a relative error of at most 0.0003.
Values sent between devices are 32-bit elements; how exact they have to be, the bound alone decides.
No kernel may reach another device: no remote copies, remote signals or barrier semaphores. Data moves between devices by JAX's collectives and lax.ppermute only.
A program may use at most 128 MiB of HBM per device.

v0:
```python
import math

import jax
import jax.numpy as jnp
from jax import lax
from jax.sharding import PartitionSpec as P

broadening = 0.25
energy_low = -3.0
energy_high = 3.0


def entering(part, axis, combine, identity, reverse):
    count = lax.axis_size(axis)
    place = lax.axis_index(axis)
    ahead = count - 1 - place if reverse else place
    gathered = jax.tree.map(lambda a: lax.all_gather(a, axis), part)
    state = jax.tree.map(lambda a, e: jnp.zeros_like(a) + jnp.asarray(e, a.dtype), part, identity)

    def one(turn, state):
        source = count - 1 - turn if reverse else turn
        return combine(
            state, jax.tree.map(lambda a: lax.dynamic_index_in_dim(a, source, 0, False), gathered)
        )

    return lax.fori_loop(0, ahead, one, state)


def matrix_product(left_factor, right_factor):
    return jnp.matmul(left_factor, right_factor, precision=lax.Precision.HIGHEST)


def complex_product(left_factor, right_factor):
    first_term = matrix_product(left_factor[0], right_factor[0])
    second_term = matrix_product(left_factor[1], right_factor[1])
    third_term = matrix_product(left_factor[0] + left_factor[1], right_factor[0] + right_factor[1])
    return jnp.stack([first_term - second_term, third_term - first_term - second_term])


def adjoint(matrix):
    return jnp.stack([jnp.swapaxes(matrix[0], -1, -2), -jnp.swapaxes(matrix[1], -1, -2)])


def invert_one(matrix):
    orbitals = matrix.shape[-1]
    conjugate = adjoint(matrix)
    normal = complex_product(conjugate, matrix)
    upper_half = jnp.concatenate([normal[0], -normal[1]], axis=1)
    lower_half = jnp.concatenate([normal[1], normal[0]], axis=1)
    factor = jnp.linalg.cholesky(jnp.concatenate([upper_half, lower_half], axis=0))
    right_side = jnp.concatenate([conjugate[0], conjugate[1]], axis=0)
    solved = jax.scipy.linalg.cho_solve((factor, True), right_side)
    return jnp.stack([solved[:orbitals], solved[orbitals:]])


def invert(matrix):
    dimensions = matrix.shape
    flattened = matrix.reshape((2, -1) + dimensions[-2:])
    result = jax.vmap(invert_one, in_axes=1, out_axes=1)(flattened)
    return result.reshape(dimensions)


def identity_for(matrix):
    orbitals = matrix.shape[-1]
    real_part = jnp.broadcast_to(jnp.eye(orbitals, dtype=jnp.float32), matrix.shape[1:])
    return jnp.stack([real_part, jnp.zeros(matrix.shape[1:], jnp.float32)])


def compose(earlier, later):
    alpha_one, beta_one, gamma_one, delta_one = earlier
    alpha_two, beta_two, gamma_two, delta_two = later
    kernel = invert(identity_for(delta_one) - complex_product(delta_one, alpha_two))
    kernel_gamma = complex_product(kernel, gamma_one)
    alpha_new = alpha_one + complex_product(beta_one, complex_product(alpha_two, kernel_gamma))
    gamma_new = complex_product(gamma_two, kernel_gamma)
    middle = beta_two + complex_product(
        alpha_two, complex_product(kernel, complex_product(delta_one, beta_two))
    )
    beta_new = complex_product(beta_one, middle)
    delta_new = delta_two + complex_product(gamma_two, complex_product(delta_one, middle))
    return (alpha_new, beta_new, gamma_new, delta_new)


def forward_transform(cosine_part, sine_part, values):
    real_part = matrix_product(cosine_part, values[0]) + matrix_product(sine_part, values[1])
    imag_part = matrix_product(cosine_part, values[1]) - matrix_product(sine_part, values[0])
    return (real_part, imag_part)


def local(onsite, hopping, sigma_prior, screened):
    blocks = onsite.shape[1]
    orbitals = onsite.shape[-1]
    per_device = sigma_prior.shape[1]
    space_count = lax.axis_size("space")
    space_rank = lax.axis_index("space")
    energy_count = lax.axis_size("energy")
    energy_rank = lax.axis_index("energy")
    total_energy = per_device * energy_count
    chain_blocks = blocks * space_count
    levels = (energy_rank * per_device + jnp.arange(per_device)).astype(jnp.float32)
    energies = energy_low + (energy_high - energy_low) * (levels + 0.5) / total_energy
    identity = jnp.eye(orbitals, dtype=jnp.float32)
    system = jnp.stack(
        [
            energies[:, None, None, None] * identity - onsite[0][None] - sigma_prior[0],
            broadening * identity - onsite[1][None] - sigma_prior[1],
        ]
    )
    global_block = space_rank * blocks + jnp.arange(blocks)
    active = (global_block < chain_blocks - 1).astype(jnp.float32)
    coupling = hopping * active[None, :, None, None]
    nothing = jnp.zeros((2, per_device, orbitals, orbitals), jnp.float32)
    left_total = None
    right_total = None
    for position in range(blocks):
        inverse = invert(system[:, :, position])
        hop_here = coupling[:, position]
        forward = complex_product(inverse, hop_here)
        backward = complex_product(adjoint(hop_here), inverse)
        closed = complex_product(backward, hop_here)
        left_piece = (inverse, forward, backward, closed)
        right_piece = (closed, backward, forward, inverse)
        if position == 0:
            left_total = left_piece
            right_total = right_piece
        else:
            left_total = compose(left_total, left_piece)
            right_total = compose(right_piece, right_total)
    unit = identity_for(nothing)
    neutral = (nothing, unit, unit, nothing)
    prefix = entering(
        (left_total[0], left_total[1], left_total[2], left_total[3]),
        "space",
        compose,
        neutral,
        False,
    )
    suffix = entering(
        (right_total[0], right_total[1], right_total[2], right_total[3]),
        "space",
        compose,
        neutral,
        True,
    )
    incoming_left = prefix[3]
    incoming_right = suffix[3]
    left_parts = [incoming_left]
    inverse = invert(system[:, :, 0] - left_parts[-1])
    hop_here = coupling[:, 0]
    left_parts.append(complex_product(complex_product(adjoint(hop_here), inverse), hop_here))
    right_parts = [nothing] * blocks
    final_coupling = coupling[:, blocks - 1]
    right_parts[blocks - 1] = complex_product(
        complex_product(final_coupling, incoming_right), adjoint(final_coupling)
    )
    inverse = invert(system[:, :, 1] - right_parts[1])
    hop_before = coupling[:, 0]
    right_parts[0] = complex_product(complex_product(hop_before, inverse), adjoint(hop_before))
    green_list = [
        invert(system[:, :, position] - left_parts[position] - right_parts[position])
        for position in range(blocks)
    ]
    green_blocks = jnp.stack(green_list, axis=2).reshape(
        2, per_device, blocks * orbitals * orbitals
    )
    gathered = lax.all_to_all(green_blocks, "energy", split_axis=2, concat_axis=1, tiled=True)
    lag_count = screened.shape[1]
    frequency = jnp.arange(lag_count)
    phase_index = frequency[:, None] * frequency[None, :] % lag_count
    phases = 2.0 * math.pi / lag_count * phase_index.astype(jnp.float32)
    cosine = jnp.cos(phases)
    sine_table = jnp.sin(phases)
    green_real, green_imag = forward_transform(
        cosine[:, :total_energy], sine_table[:, :total_energy], gathered
    )
    screen_real, screen_imag = forward_transform(cosine, sine_table, screened)
    spectrum_real = green_real * screen_real - green_imag * screen_imag
    spectrum_imag = green_real * screen_imag + green_imag * screen_real
    back_cosine = cosine[:total_energy]
    back_sine = sine_table[:total_energy]
    result_real = (
        matrix_product(back_cosine, spectrum_real) - matrix_product(back_sine, spectrum_imag)
    ) / lag_count
    result_imag = (
        matrix_product(back_cosine, spectrum_imag) + matrix_product(back_sine, spectrum_real)
    ) / lag_count
    return jnp.stack([result_real, result_imag])


def solution(mesh):
    in_specs = (
        P(None, "space", None, None),
        P(None, "space", None, None),
        P(None, "energy", "space", None, None),
        P(None, None, ("space", "energy")),
    )
    out_specs = P(None, None, ("space", "energy"))
    return jax.shard_map(local, mesh=mesh, in_specs=in_specs, out_specs=out_specs, check_vma=False)
```

profile of v0, /device:TPU:5, one launch (start us, length us, event | category | flops | bytes accessed | tf_op | source)
XLA Modules:
  0.0 645.5 jit_solution(9345196476339403676)
XLA Ops:
  0.0 1.0 fusion.339
  2.6 11.7 %custom-call.45 = f32[1,128,128]{2,1,0:T(8,128)S(1)} custom-call(f32[1,128,128]{2,1,0:T(8,128)S(1)} %fusion.334), custom_call_target="Cholesky" | custom-call | tf_op jit(solution)/shard_map/vmap(jit(cholesky))/cholesky/custom-call.1 | solution.py:50
  14.3 0.6 compare_reduce_fusion.8
  15.0 0.7 fusion.295
  15.6 9.8 %custom-call.47 = f32[1,1,128,128]{2,3,1,0:T(8,128)S(1)} custom-call(f32[1,1,128,128]{3,2,1,0:T(8,128)S(1)} %fusion.295), custom_call_target="InvertDiagBlocksLowerTriangular" | custom-call | tf_op jit(solution)/shard_map/vmap(jit(_cho_solve))/triangular_solve/custom-call.2 | solution.py:52
  25.9 1.0 broadcast_multiply_fusion
  28.0 11.7 %custom-call.42 = f32[1,128,128]{2,1,0:T(8,128)S(1)} custom-call(f32[1,128,128]{2,1,0:T(8,128)S(1)} %fusion.338), custom_call_target="Cholesky" | custom-call | tf_op jit(solution)/shard_map/vmap(jit(cholesky))/cholesky/custom-call.1 | solution.py:50
  39.7 0.6 compare_reduce_fusion.9
  40.4 0.7 fusion.294
  41.0 10.0 %custom-call.44 = f32[1,1,128,128]{2,3,1,0:T(8,128)S(1)} custom-call(f32[1,1,128,128]{3,2,1,0:T(8,128)S(1)} %fusion.294), custom_call_target="InvertDiagBlocksLowerTriangular" | custom-call | tf_op jit(solution)/shard_map/vmap(jit(_cho_solve))/triangular_solve/custom-call.2 | solution.py:52
  56.1 11.7 %custom-call.48 = f32[1,128,128]{2,1,0:T(8,128)S(1)} custom-call(f32[1,128,128]{2,1,0:T(8,128)S(1)} %fusion.330), custom_call_target="Cholesky" | custom-call | tf_op jit(solution)/shard_map/vmap(jit(cholesky))/cholesky/custom-call.1 | solution.py:50
  67.9 0.6 compare_reduce_fusion.7
  68.5 0.7 fusion.296
  69.2 9.8 %custom-call.50 = f32[1,1,128,128]{2,3,1,0:T(8,128)S(1)} custom-call(f32[1,1,128,128]{3,2,1,0:T(8,128)S(1)} %fusion.296), custom_call_target="InvertDiagBlocksLowerTriangular" | custom-call | tf_op jit(solution)/shard_map/vmap(jit(_cho_solve))/triangular_solve/custom-call.2 | solution.py:52
  84.0 12.1 %custom-call.51 = f32[1,128,128]{2,1,0:T(8,128)S(1)} custom-call(f32[1,128,128]{2,1,0:T(8,128)S(1)} %fusion.326), custom_call_target="Cholesky" | custom-call | tf_op jit(solution)/shard_map/vmap(jit(cholesky))/cholesky/custom-call.1 | solution.py:50
  96.2 0.6 compare_reduce_fusion.6
  96.8 0.7 fusion.297
  97.5 9.8 %custom-call.53 = f32[1,1,128,128]{2,3,1,0:T(8,128)S(1)} custom-call(f32[1,1,128,128]{3,2,1,0:T(8,128)S(1)} %fusion.297), custom_call_target="InvertDiagBlocksLowerTriangular" | custom-call | tf_op jit(solution)/shard_map/vmap(jit(_cho_solve))/triangular_solve/custom-call.2 | solution.py:52
  119.7 6.3 all_gather.51
  126.0 5.9 all-gather.3
  131.9 5.9 all-gather.2
  137.8 5.9 all_gather.46
  143.7 6.6 %while.33 = (s32[]{:T(128)}, f32[2,1,64,64]{3,2,1,0:T(8,128)S(1)}, s32[]{:T(128)}, f32[4,2,1,64,64]{4,3,1,2,0:T(8,128)S(1)}, f32[4,2,1,64,64]{4,3,2,1,0:T(8,128)...) while((s32[]{:T(128)}, f32[2,1,64,64]{3,2,1,0:T(8,128)S(1)}, ...), condition=%wide.region_5.9_spmd, body=%wide.region_4.8_spmd.sunk | while | flops 91713664 | bytes 4072713 | solution.py:26
  152.5 11.7 %custom-call.54 = f32[1,128,128]{2,1,0:T(8,128)S(1)} custom-call(f32[1,128,128]{2,1,0:T(8,128)S(1)} %fusion.322), custom_call_target="Cholesky" | custom-call | tf_op jit(solution)/shard_map/vmap(jit(cholesky))/cholesky/custom-call.1 | solution.py:50
  164.2 0.6 compare_reduce_fusion.5
  164.9 0.7 fusion.298
  165.5 9.8 %custom-call.56 = f32[1,1,128,128]{2,3,1,0:T(8,128)S(1)} custom-call(f32[1,1,128,128]{3,2,1,0:T(8,128)S(1)} %fusion.298), custom_call_target="InvertDiagBlocksLowerTriangular" | custom-call | tf_op jit(solution)/shard_map/vmap(jit(_cho_solve))/triangular_solve/custom-call.2 | solution.py:52
  177.2 84.4 %all-gather.1 = f32[8,1,64,64]{3,2,1,0:T(8,128)S(1)} all-gather(f32[2,1,64,64]{3,2,1,0:T(8,128)S(1)} %pad_maximum_fusion.4), channel_id=3, replica_groups=mesh['space'=4,'energy'=8] {'space'}, dimensions={0}, use_global_device_ids=true | all-gather | bytes 163840 | tf_op jit(solution)/shard_map/all_gather | solution.py:17
  261.6 5.9 all-gather
  267.4 5.8 all_gather.40
  273.4 5.9 all_gather.45
  279.2 86.3 %while.32 = (s32[]{:T(128)}, f32[2,1,64,64]{3,2,1,0:T(8,128)S(1)}, s32[]{:T(128)}, f32[4,2,1,64,64]{4,3,1,2,0:T(8,128)S(1)}, f32[4,2,1,64,64]{4,3,2,1,0:T(8,128)...) while((s32[]{:T(128)}, f32[2,1,64,64]{3,2,1,0:T(8,128)S(1)}, ...), condition=%wide.region_3.7_spmd, body=%wide.region_2.6_spmd.sunk | while | flops 91713664 | bytes 4072693 | solution.py:26
  281.2 11.7 %custom-call.70 = f32[1,128,128]{2,1,0:T(8,128)S(1)} custom-call(f32[1,128,128]{2,1,0:T(8,128)S(1)} %fusion.1084), custom_call_target="Cholesky" | custom-call | tf_op jit(solution)/shard_map/while/body/vmap(jit(cholesky))/cholesky/custom-call.1 | solution.py:50
  293.0 0.6 compare_reduce_fusion.12
  293.6 0.7 fusion.1085
  294.3 9.8 %custom-call.71 = f32[1,1,128,128]{2,3,1,0:T(8,128)S(1)} custom-call(f32[1,1,128,128]{3,2,1,0:T(8,128)S(1)} %fusion.1085), custom_call_target="InvertDiagBlocksLowerTriangular" | custom-call | tf_op jit(solution)/shard_map/while/body/vmap(jit(_cho_solve))/triangular_solve/custom-call.2 | solution.py:52
  309.8 11.7 %custom-call.70 = f32[1,128,128]{2,1,0:T(8,128)S(1)} custom-call(f32[1,128,128]{2,1,0:T(8,128)S(1)} %fusion.1084), custom_call_target="Cholesky" | custom-call | tf_op jit(solution)/shard_map/while/body/vmap(jit(cholesky))/cholesky/custom-call.1 | solution.py:50
  321.6 0.6 compare_reduce_fusion.12
  322.2 0.7 fusion.1085
  322.9 9.8 %custom-call.71 = f32[1,1,128,128]{2,3,1,0:T(8,128)S(1)} custom-call(f32[1,1,128,128]{3,2,1,0:T(8,128)S(1)} %fusion.1085), custom_call_target="InvertDiagBlocksLowerTriangular" | custom-call | tf_op jit(solution)/shard_map/while/body/vmap(jit(_cho_solve))/triangular_solve/custom-call.2 | solution.py:52
  338.4 11.7 %custom-call.70 = f32[1,128,128]{2,1,0:T(8,128)S(1)} custom-call(f32[1,128,128]{2,1,0:T(8,128)S(1)} %fusion.1084), custom_call_target="Cholesky" | custom-call | tf_op jit(solution)/shard_map/while/body/vmap(jit(cholesky))/cholesky/custom-call.1 | solution.py:50
  350.1 0.6 compare_reduce_fusion.12
  350.8 0.7 fusion.1085
  351.4 9.8 %custom-call.71 = f32[1,1,128,128]{2,3,1,0:T(8,128)S(1)} custom-call(f32[1,1,128,128]{3,2,1,0:T(8,128)S(1)} %fusion.1085), custom_call_target="InvertDiagBlocksLowerTriangular" | custom-call | tf_op jit(solution)/shard_map/while/body/vmap(jit(_cho_solve))/triangular_solve/custom-call.2 | solution.py:52
  367.4 11.7 %custom-call.60 = f32[1,128,128]{2,1,0:T(8,128)S(1)} custom-call(f32[1,128,128]{2,1,0:T(8,128)S(1)} %fusion.314), custom_call_target="Cholesky" | custom-call | tf_op jit(solution)/shard_map/vmap(jit(cholesky))/cholesky/custom-call.1 | solution.py:50
  379.1 0.6 compare_reduce_fusion.3
  379.8 0.7 fusion.300
  380.4 9.8 %custom-call.62 = f32[1,1,128,128]{2,3,1,0:T(8,128)S(1)} custom-call(f32[1,1,128,128]{3,2,1,0:T(8,128)S(1)} %fusion.300), custom_call_target="InvertDiagBlocksLowerTriangular" | custom-call | tf_op jit(solution)/shard_map/vmap(jit(_cho_solve))/triangular_solve/custom-call.2 | solution.py:52
  393.1 11.7 %custom-call.57 = f32[1,128,128]{2,1,0:T(8,128)S(1)} custom-call(f32[1,128,128]{2,1,0:T(8,128)S(1)} %fusion.318), custom_call_target="Cholesky" | custom-call | tf_op jit(solution)/shard_map/vmap(jit(cholesky))/cholesky/custom-call.1 | solution.py:50
  404.9 0.6 compare_reduce_fusion.4
  405.5 0.7 fusion.299
  406.2 10.0 %custom-call.59 = f32[1,1,128,128]{2,3,1,0:T(8,128)S(1)} custom-call(f32[1,1,128,128]{3,2,1,0:T(8,128)S(1)} %fusion.299), custom_call_target="InvertDiagBlocksLowerTriangular" | custom-call | tf_op jit(solution)/shard_map/vmap(jit(_cho_solve))/triangular_solve/custom-call.2 | solution.py:52
  417.0 11.7 %custom-call.63 = f32[1,128,128]{2,1,0:T(8,128)S(1)} custom-call(f32[1,128,128]{2,1,0:T(8,128)S(1)} %fusion.310), custom_call_target="Cholesky" | custom-call | tf_op jit(solution)/shard_map/vmap(jit(cholesky))/cholesky/custom-call.1 | solution.py:50
  428.8 0.6 compare_reduce_fusion.2
  429.4 0.7 fusion.301
  430.1 9.8 %custom-call.65 = f32[1,1,128,128]{2,3,1,0:T(8,128)S(1)} custom-call(f32[1,1,128,128]{3,2,1,0:T(8,128)S(1)} %fusion.301), custom_call_target="InvertDiagBlocksLowerTriangular" | custom-call | tf_op jit(solution)/shard_map/vmap(jit(_cho_solve))/triangular_solve/custom-call.2 | solution.py:52
  440.5 4.9 copy.402
  445.9 38.3 %reduce.111 = f32[8192,2]{1,0:T(8,128)} reduce(f32[8192,1,2]{2,1,0:T(1,128)} %bitcast.1517, f32[]{:T(128)} %broadcast.248), dimensions={1}, to_apply=%bitcast.1141.reduce_sub_computation | reduce | bytes 131076
  484.2 5.2 reshape.2147
  489.4 5.5 all-to-all-start
  496.2 4.5 all-to-all-done
  500.7 0.7 reduce.112
  501.4 8.3 %reshape.2148 = f32[8192,1,2]{2,1,0:T(1,128)} reshape(f32[8,2048]{1,0:T(8,128)S(1)} %reduce.112) | data formatting | bytes 131072
  509.7 133.4 %slice_reduce_fusion.1 = (f32[8192]{0:T(1024)S(1)}, f32[8192]{0:T(1024)S(1)}) fusion(f32[2,1,8192]{0,1,2:T(1,128)} %bitcast.1516), kind=kLoop, calls=%fused_computation.303 | loop fusion | bytes 131072 | tf_op jit(solution)/shard_map/slice | solution.py:85
  (371 shorter events, 54.9 us)
Async XLA Ops:
  484.2 10.7 %copy-start = (f32[2,15,1024]{2,0,1:T(2,128)S(1)}, f32[2,15,1024]{2,0,1:T(2,128)}, u32[]{:S(2)}) copy-start(f32[2,15,1024]{2,0,1:T(2,128)} %param.16) | copy-start | bytes 368644
  489.4 11.3 %all-to-all-start = ((f32[8,1,2048]{2,1,0:T(1,128)}), f32[8,1,2048]{2,1,0:T(1,128)S(1)}, u32[]{:S(2)}, u32[]{:S(2)}) async-start(f32[8,1,2048]{2,1,0:T(1,128)} %reshape.2147), calls=%async_computation | async-start | bytes 131072 | tf_op jit(solution)/shard_map/all_to_all | solution.py:166
where the time goes:
time: 655 us; the launch traced here: 645 us
  other arithmetic  297 us (45%)
  local copies, waits for them, and re-layouts  154 us (24%)
  blocking collectives  126 us (19%)
  matrix products  49 us (7%)
  loops' own time  8.09 us (1%)
    another operation x33, other arithmetic, invert_one(): jnp.linalg.cholesky(jnp.concatenate([upper_half, lower_half], axis=0))  137 us
    slice x1, local copies, waits for them, and re-layouts, forward_transform(): values[0]  133 us
    all_gather x8, blocking collectives, entering(): gathered = jax.tree.map(lambda a: lax.all_gather(a, axis), part)  126 us
    another operation x22, other arithmetic, invert_one(): solved = jax.scipy.linalg.cho_solve((factor, True), right_side)  115 us
    dot_general x201, matrix products, matrix_product(): jnp.matmul(left_factor, right_factor, precision=lax.Precision.HIGHEST)  43.7 us
    unnamed x1, other arithmetic  38.3 us
    unnamed x5, local copies, waits for them, and re-layouts  14 us
  transfers between devices with their start and end apart: 1, of which 1 were waited for; matrix products, arithmetic and copies ran while one was open for 0% of the time, Pallas kernels for 0%

commit v1 on v0

v1 whole, which is shorter than its diff:
```python
import functools

import jax
import jax.numpy as jnp
from jax import lax
from jax.experimental import pallas as pl
from jax.experimental.pallas import tpu as pltpu
from jax.sharding import PartitionSpec as P

broadening = 0.25
energy_low = -3.0
energy_high = 3.0

PANEL = 8
SMALL = 2.0**-64
LARGE = 2.0**120


def iota(shape, dim):
    return lax.broadcasted_iota(jnp.int32, shape, dim)


def swap_halves(x):
    return pltpu.roll(x, x.shape[1] // 2, 1)


def low_half(x):
    return iota(x.shape, 1) < x.shape[1] // 2


def lane_broadcast(x, column):
    half = x.shape[1] // 2
    index = (iota(x.shape, 1) & half) + column
    return jnp.take_along_axis(x, index, axis=1, mode="promise_in_bounds")


def sublane_broadcast(x, row):
    return jnp.broadcast_to(x[row : row + 1, :], x.shape)


def complex_reciprocal(real, imag):
    square = real * real + imag * imag
    factor = 1.0 / square
    real_small, imag_small = real * SMALL, imag * SMALL
    factor_small = SMALL / (real_small * real_small + imag_small * imag_small)
    plain = square < LARGE
    return (
        jnp.where(plain, real * factor, real_small * factor_small),
        -jnp.where(plain, imag * factor, imag_small * factor_small),
    )


def invert_block(real, imag):
    real, imag = list(real), list(imag)
    sub = iota(real[0].shape, 0)
    for step in range(PANEL):
        here = sub == step
        pivot_real = sublane_broadcast(real[step], step)
        pivot_imag = sublane_broadcast(imag[step], step)
        recip_real, recip_imag = complex_reciprocal(pivot_real, pivot_imag)
        mult_real = real[step] * recip_real - imag[step] * recip_imag
        mult_imag = real[step] * recip_imag + imag[step] * recip_real
        mult_real = jnp.where(here, -recip_real, mult_real)
        mult_imag = jnp.where(here, -recip_imag, mult_imag)
        for other in range(PANEL):
            if other == step:
                continue
            row_real = sublane_broadcast(real[other], step)
            row_imag = sublane_broadcast(imag[other], step)
            rest_real = jnp.where(here, 0.0, real[other])
            rest_imag = jnp.where(here, 0.0, imag[other])
            real[other] = rest_real - mult_real * row_real + mult_imag * row_imag
            imag[other] = rest_imag - mult_real * row_imag - mult_imag * row_real
        real[step], imag[step] = -mult_real, -mult_imag
    return real, imag


def eliminate_panel(real, imag, panel):
    half = real[0].shape[1] // 2
    lane = iota(real[0].shape, 1) & (half - 1)
    inside = (lane // PANEL) == panel
    unit = jnp.where((lane & (PANEL - 1)) == iota(real[0].shape, 0), 1.0, 0.0)

    def columns(group):
        return (
            [lane_broadcast(real[group], panel * PANEL + c) for c in range(PANEL)],
            [lane_broadcast(imag[group], panel * PANEL + c) for c in range(PANEL)],
        )

    inverse_real, inverse_imag = invert_block(*columns(panel))
    top_real = jnp.where(inside, unit, real[panel])
    top_imag = jnp.where(inside, 0.0, imag[panel])
    row_real = row_imag = None
    for c in range(PANEL):
        a, b = sublane_broadcast(top_real, c), sublane_broadcast(top_imag, c)
        term_real = inverse_real[c] * a - inverse_imag[c] * b
        term_imag = inverse_real[c] * b + inverse_imag[c] * a
        row_real = term_real if row_real is None else row_real + term_real
        row_imag = term_imag if row_imag is None else row_imag + term_imag
    spread_real = [sublane_broadcast(row_real, c) for c in range(PANEL)]
    spread_imag = [sublane_broadcast(row_imag, c) for c in range(PANEL)]
    new_real, new_imag = list(real), list(imag)
    for ahead in range(1, len(real)):
        group = (panel + ahead) % len(real)
        column_real, column_imag = columns(group)
        a = jnp.where(inside, 0.0, real[group])
        b = jnp.where(inside, 0.0, imag[group])
        for c in range(PANEL):
            a = a - column_real[c] * spread_real[c] + column_imag[c] * spread_imag[c]
            b = b - column_real[c] * spread_imag[c] - column_imag[c] * spread_real[c]
        new_real[group], new_imag[group] = a, b
    new_real[panel], new_imag[panel] = row_real, row_imag
    return new_real, new_imag


def invert_pair(first, second):
    low = low_half(first)
    real = jnp.where(low, first, swap_halves(second))
    imag = jnp.where(low, swap_halves(first), second)
    groups = first.shape[0] // PANEL
    real = [real[PANEL * g : PANEL * (g + 1)] for g in range(groups)]
    imag = [imag[PANEL * g : PANEL * (g + 1)] for g in range(groups)]
    for panel in range(groups):
        real, imag = eliminate_panel(real, imag, panel)
    return jnp.concatenate(real, 0), jnp.concatenate(imag, 0)


def side_of_pair(real, imag):
    low = low_half(real)
    return jnp.where(low, real, swap_halves(imag)), jnp.where(low, swap_halves(real), imag)


def times_i(x):
    turned = swap_halves(x)
    return jnp.where(low_half(x), -turned, turned)


def matmul(a, b):
    a_high, b_high = a.astype(jnp.bfloat16), b.astype(jnp.bfloat16)
    a_low = (a - a_high.astype(jnp.float32)).astype(jnp.bfloat16)
    b_low = (b - b_high.astype(jnp.float32)).astype(jnp.bfloat16)
    return jnp.dot(
        jnp.concatenate([a_high, a_high, a_low], 1),
        jnp.concatenate([b_high, b_low, b_high], 0),
        preferred_element_type=jnp.float32,
    )


def pair_solve(real, imag, right_first, right_second):
    low = low_half(real)
    left = jnp.concatenate(
        [
            jnp.concatenate([jnp.where(low, real, 0.0), jnp.where(low, imag, 0.0)], 1),
            jnp.concatenate([jnp.where(low, 0.0, real), jnp.where(low, 0.0, imag)], 1),
        ],
        0,
    )
    rows = real.shape[0]
    firsts, seconds = [], []
    for a, b in zip(right_first, right_second):
        stacked = jnp.concatenate([a, b], 0)
        turned = times_i(stacked)
        right = jnp.concatenate(
            [
                jnp.concatenate([stacked, turned], 1),
                jnp.concatenate([turned, -stacked], 1),
            ],
            0,
        )
        product = matmul(left, right)
        width = stacked.shape[1]
        firsts.append(jnp.concatenate([product[:rows, :width], product[:rows, width:]], 0))
        seconds.append(jnp.concatenate([product[rows:, :width], product[rows:, width:]], 0))
    return jnp.concatenate(firsts, 1), jnp.concatenate(seconds, 1)


def eliminate(block_first, block_second, sides_first, sides_second):
    real, imag = invert_pair(block_first, block_second)
    right_first, right_second = pair_solve(
        real,
        imag,
        [sides_first[1], sides_first[2]],
        [sides_second[1], sides_second[2]],
    )
    results = []
    for sides, right in ((sides_first, right_first), (sides_second, right_second)):
        rows, width = sides[0].shape
        out = matmul(jnp.concatenate([sides[0], sides[3]], 0), right)
        results.append(
            (out[:rows, :width], out[:rows, width:], out[rows:, :width], out[rows:, width:])
        )
    return results


def adjoint(x):
    half = x.shape[1] // 2
    turned = x.T
    return jnp.concatenate([turned[:half], -turned[half:]], 1)


def reduce_kernel(
    energy_ref, onsite_ref, hopping_ref, sigma_ref, own_ref, reduced_ref
):
    orbitals = onsite_ref.shape[-1]
    energy, active = energy_ref[0], energy_ref[1]
    unit = jnp.where(
        iota((orbitals, orbitals), 0) == iota((orbitals, orbitals), 1), 1.0, 0.0
    )
    system = [
        jnp.concatenate(
            [
                energy * unit - onsite_ref[0, n] - sigma_ref[0, n],
                broadening * unit - onsite_ref[1, n] - sigma_ref[1, n],
            ],
            1,
        )
        for n in range(2)
    ]
    within = jnp.concatenate([hopping_ref[0, 0], hopping_ref[1, 0]], 1)
    beyond = jnp.concatenate([hopping_ref[0, 1], hopping_ref[1, 1]], 1) * active
    within_adjoint, beyond_adjoint = adjoint(within), adjoint(beyond)
    own_ref[0], own_ref[1] = system
    own_ref[2], own_ref[3] = within, within_adjoint
    own_ref[4], own_ref[5] = beyond, beyond_adjoint
    sides = (within, within_adjoint, beyond, beyond_adjoint)
    products, unused = eliminate(system[1], system[1], sides, sides)
    reduced_ref[0] = system[0] - products[0]
    reduced_ref[1] = products[3]
    reduced_ref[2] = -products[1]
    reduced_ref[3] = -products[2]


def solve_kernel(count, own_ref, *refs):
    others, green_ref = refs[:-1], refs[-1]
    even, odd = own_ref[0], own_ref[1]
    within, within_adjoint = own_ref[2], own_ref[3]
    blocks = {turn: others[turn - 1][0] for turn in range(1, count)}
    for turn in range(1, count - 1):
        blocks[turn + 1] = blocks[turn + 1] - others[turn - 1][1]
    blocks[0] = odd
    blocks[count] = even - others[count - 2][1]
    links = {turn: (others[turn - 1][2], others[turn - 1][3]) for turn in range(1, count)}
    links[0] = (-own_ref[4], -own_ref[5])
    stride = 1
    while stride < count:
        turns = list(range(stride, count, 2 * stride))
        last = len(turns) == 1
        for start in range(0, len(turns), 2):
            chosen = turns[start : start + 2]
            both = chosen if len(chosen) == 2 else chosen * 2
            sides = [links[t - stride] + links[t] for t in both]
            results = eliminate(blocks[both[0]], blocks[both[1]], sides[0], sides[1])
            for t, (left_left, left_right, right_left, right_right) in zip(chosen, results):
                blocks[t - stride] = blocks[t - stride] - left_left
                blocks[t + stride] = blocks[t + stride] - right_right
                if not last:
                    links[t - stride] = (-left_right, -right_left)
        stride *= 2
    even, odd = blocks[count], blocks[0]
    real, imag = invert_pair(even, odd)
    right_even, right_odd = pair_solve(real, imag, [within], [within_adjoint])
    odd_new = odd - matmul(within_adjoint, right_even)
    even_new = even - matmul(within, right_odd)
    real, imag = invert_pair(even_new, odd_new)
    rows = even.shape[0]
    green_ref[:rows], green_ref[rows:] = side_of_pair(real, imag)


def convolve_kernel(green_ref, screened_ref, out_ref, lag_ref):
    energies, rows, width = green_ref.shape
    lags = screened_ref.shape[1]
    half = width // 2
    for part in range(2):
        lag_ref[part, : lags - energies] = screened_ref[part, energies:]
        lag_ref[part, lags - energies : lags] = screened_ref[part, :energies]
    low = iota((energies, width), 1) < half
    for tile in range(rows // 2):
        place = pl.ds(tile * width, width)
        first, second = green_ref[:, 2 * tile, :], green_ref[:, 2 * tile + 1, :]
        real = jnp.where(low, first, swap_halves(second))
        imag = jnp.where(low, swap_halves(first), second)
        out_real = jnp.zeros((energies, width), jnp.float32)
        out_imag = jnp.zeros((energies, width), jnp.float32)
        for source in range(energies):
            window = pl.ds(lags - energies - source, energies)
            screen_real, screen_imag = lag_ref[0, window, place], lag_ref[1, window, place]
            a = jnp.broadcast_to(real[source : source + 1], (energies, width))
            b = jnp.broadcast_to(imag[source : source + 1], (energies, width))
            out_real = out_real + a * screen_real - b * screen_imag
            out_imag = out_imag + a * screen_imag + b * screen_real
        out_ref[0, :, place] = out_real
        out_ref[1, :, place] = out_imag


def local(onsite, hopping, sigma_prior, screened):
    blocks, orbitals = onsite.shape[1], onsite.shape[-1]
    space_count = lax.axis_size("space")
    energy_count = lax.axis_size("energy")
    if blocks != 2 or sigma_prior.shape[1] != 1 or space_count & (space_count - 1):
        raise ValueError("unsupported placement")
    width = 2 * orbitals
    side = jax.ShapeDtypeStruct((orbitals, width), jnp.float32)
    level = lax.axis_index("energy").astype(jnp.float32)
    energy = energy_low + (energy_high - energy_low) * (level + 0.5) / energy_count
    active = (lax.axis_index("space") < space_count - 1).astype(jnp.float32)
    whole = pl.BlockSpec(memory_space=pltpu.VMEM)
    own, reduced = pl.pallas_call(
        reduce_kernel,
        out_shape=(
            jax.ShapeDtypeStruct((6,) + side.shape, jnp.float32),
            jax.ShapeDtypeStruct((4,) + side.shape, jnp.float32),
        ),
        in_specs=[pl.BlockSpec(memory_space=pltpu.SMEM), whole, whole, whole],
        out_specs=(whole, whole),
    )(jnp.stack([energy, active]), onsite, hopping, sigma_prior.reshape(onsite.shape))
    others = [
        lax.ppermute(
            reduced,
            "space",
            [((r + turn) % space_count, r) for r in range(space_count)],
        )
        for turn in range(1, space_count)
    ]
    green = pl.pallas_call(
        functools.partial(solve_kernel, space_count),
        out_shape=jax.ShapeDtypeStruct((blocks * orbitals, width), jnp.float32),
        in_specs=[whole] * space_count,
        out_specs=whole,
    )(own, *others)
    pieces = green.reshape(energy_count, blocks * orbitals // energy_count, width)
    gathered = lax.all_to_all(pieces, "energy", split_axis=0, concat_axis=0, tiled=True)
    lag_count, entries = screened.shape[1:]
    return pl.pallas_call(
        convolve_kernel,
        out_shape=jax.ShapeDtypeStruct((2, energy_count, entries), jnp.float32),
        in_specs=[whole, whole],
        out_specs=whole,
        scratch_shapes=[pltpu.VMEM((2, lag_count + 1, entries), jnp.float32)],
    )(gathered, screened)


def solution(mesh):
    in_specs = (
        P(None, "space", None, None),
        P(None, "space", None, None),
        P(None, "energy", "space", None, None),
        P(None, None, ("space", "energy")),
    )
    out_specs = P(None, None, ("space", "energy"))
    return jax.shard_map(local, mesh=mesh, in_specs=in_specs, out_specs=out_specs, check_vma=False)
```

time: 655 us -> 47.6 us (0.07)
  the two profiles are of different devices: /device:TPU:5 before, /device:TPU:0 now
where the time goes in v1:
time: 47.6 us; the launch traced here: 47.4 us
  Pallas kernels  22.3 us (47%)
  waiting for transfers between devices  13.2 us (28%)
  starting transfers between devices  9.28 us (19%)
  local copies, waits for them, and re-layouts  2.01 us (4%)
  other arithmetic  0.62 us (1%)
    pallas_call x1, Pallas kernels, local(): pl.pallas_call(functools.partial(solve_kernel, space_count), out_shape=ja...  15.1 us
    ppermute x3, waiting for transfers between devices, local(): lax.ppermute(reduced, 'space', [((r + turn) % space_count, r) for r in ra...  6.96 us
    all_to_all x1, waiting for transfers between devices, local(): lax.all_to_all(pieces, 'energy', split_axis=0, concat_axis=0, tiled=True)  6.21 us
    all_to_all x1, starting transfers between devices, local(): lax.all_to_all(pieces, 'energy', split_axis=0, concat_axis=0, tiled=True)  6.06 us
    pallas_call x1, Pallas kernels, local(): pl.pallas_call(reduce_kernel, out_shape=(jax.ShapeDtypeStruct((6,) + side...  5.33 us
    ppermute x3, starting transfers between devices, local(): lax.ppermute(reduced, 'space', [((r + turn) % space_count, r) for r in ra...  3.22 us
    unnamed x11, local copies, waits for them, and re-layouts  2.01 us
    pallas_call x1, Pallas kernels, local(): pl.pallas_call(convolve_kernel, out_shape=jax.ShapeDtypeStruct((2, energy...  1.89 us
  transfers between devices with their start and end apart: 4, of which 3 were waited for; matrix products, arithmetic and copies ran while one was open for 1% of the time, Pallas kernels for 0%

profile of v1, /device:TPU:0, one launch (start us, length us, event | category | flops | bytes accessed | tf_op | source)
XLA Modules:
  0.0 47.4 jit_solution(10192351868282598352)
XLA Ops:
  0.0 0.6 %pad_maximum_fusion.energy_ref = f32[2]{0:T(128)} fusion(f32[1]{0:T(128)} %bitcast.1, f32[1]{0:T(128)} %bitcast), kind=kLoop, calls=%fused_computation | loop fusion | flops 2 | bytes 16 | tf_op jit(solution)/shard_map/stack | solution.py:315
  0.6 5.3 %shard_map.46 = (f32[6,64,128]{2,1,0:T(8,128)}, f32[4,64,128]{2,1,0:T(8,128)}) custom-call(f32[2]{0:T(128)} %pad_maximum_fusion.energy_ref, f32[2,2,64,64]{3,2,1,0:T(8,128)} %onsite_ref.1, f32[2,2,64,64]{3,2,1,0:T(8,128)} %hopping_ref.1, f32[2,2,64,64]{3,2,1,0:T(8,128)} %bitcast.5), custom_call_target="tpu_custom_call" | custom-call | tf_op jit(solution)/shard_map/pallas_call | solution.py:307
  5.9 2.4 %collective-permute-start = (f32[4,64,128]{2,1,0:T(8,128)}, f32[4,64,128]{2,1,0:T(8,128)S(1)}, u32[]{:S(2)}, u32[]{:S(2)}) collective-permute-start(f32[4,64,128]{2,1,0:T(8,128)} %get-tuple-element.8), channel_id=1, source_target_pairs={{8,0},{16,8},{24,16},{0,24},{9,1},{17,9},{25,17},{1,25},{10,2},{18... | collective-permute-start | bytes 393224 | tf_op jit(solution)/shard_map/ppermute | solution.py:317
  8.4 0.6 %collective-permute-start.1 = (f32[4,64,128]{2,1,0:T(8,128)}, f32[4,64,128]{2,1,0:T(8,128)S(1)}, u32[]{:S(2)}, u32[]{:S(2)}) collective-permute-start(f32[4,64,128]{2,1,0:T(8,128)} %get-tuple-element.8), channel_id=1, source_target_pairs={{16,0},{24,8},{0,16},{8,24},{17,1},{25,9},{1,17},{9,25},{18,2},{26... | collective-permute-start | bytes 393224 | tf_op jit(solution)/shard_map/ppermute | solution.py:317
  8.9 0.2 collective-permute-start.2
  9.2 3.3 %collective-permute-done.refs_0_ = f32[4,64,128]{2,1,0:T(8,128)S(1)} collective-permute-done((f32[4,64,128]{2,1,0:T(8,128)}, f32[4,64,128]{2,1,0:T(8,128)S(1)}, u32[]{:S(2)}, u32[]{:S(2)}) %collective-permute-start) | collective-permute-done | bytes 131104 | tf_op jit(solution)/shard_map/ppermute | solution.py:317
  12.5 0.0 copy-start.1
  12.5 3.6 %collective-permute-done.1.refs_1_ = f32[4,64,128]{2,1,0:T(8,128)S(1)} collective-permute-done((f32[4,64,128]{2,1,0:T(8,128)}, f32[4,64,128]{2,1,0:T(8,128)S(1)}, u32[]{:S(2)}, u32[]{:S(2)}) %collective-permute-start.1) | collective-permute-done | bytes 131104 | tf_op jit(solution)/shard_map/ppermute | solution.py:317
  16.1 0.0 copy-start.2
  16.1 0.0 collective-permute-done.2.refs_2_
  16.1 0.0 copy-start.3
  16.1 0.0 copy-done.1
  16.1 0.6 %copy-done.2 = f32[4,64,128]{2,1,0:T(8,128)} copy-done((f32[4,64,128]{2,1,0:T(8,128)}, f32[4,64,128]{2,1,0:T(8,128)S(1)}, u32[]{:S(2)}) %copy-start.2) | copy-done | bytes 131096
  16.8 0.1 copy-done.3
  16.8 15.1 %shard_map.47 = f32[128,128]{1,0:T(8,128)} custom-call(f32[6,64,128]{2,1,0:T(8,128)} %get-tuple-element.7.own_ref, f32[4,64,128]{2,1,0:T(8,128)} %copy-done.1, f32[4,64,128]{2,1,0:T(8,128)} %copy-done.2, f32[4,64,128]{2,1,0:T(8,128)} %copy-done.3), custom_call_target="tpu_custom_call" | custom-call | tf_op jit(solution)/shard_map/pallas_call | solution.py:324
  31.9 0.0 copy-start.4
  31.9 6.1 %all-to-all-start = ((f32[8,16,128]{2,1,0:T(8,128)}), f32[8,16,128]{2,1,0:T(8,128)S(1)}, u32[]{:S(2)}, u32[]{:S(2)}) async-start(f32[8,16,128]{2,1,0:T(8,128)} %bitcast.4), calls=%async_computation | async-start | bytes 131072 | tf_op jit(solution)/shard_map/all_to_all | solution.py:331
  38.0 0.0 copy-done.4
  38.0 0.7 %copy.5.screened_ref = f32[2,15,1024]{2,1,0:T(8,128)} copy(f32[2,15,1024]{2,0,1:T(2,128)S(1)} %copy-done.4) | data formatting | bytes 245760 | tf_op args[3]
  38.7 6.2 %all-to-all-done.green_ref = f32[8,16,128]{2,1,0:T(8,128)S(1)} async-done(((f32[8,16,128]{2,1,0:T(8,128)}), f32[8,16,128]{2,1,0:T(8,128)S(1)}, u32[]{:S(2)}, u32[]{:S(2)}) %all-to-all-start) | async-done | bytes 65568 | tf_op jit(solution)/shard_map/all_to_all | solution.py:331
  44.9 0.0 copy-start
  44.9 0.6 %copy-done = f32[8,16,128]{2,1,0:T(8,128)} copy-done((f32[8,16,128]{2,1,0:T(8,128)}, f32[8,16,128]{2,1,0:T(8,128)S(1)}, u32[]{:S(2)}) %copy-start) | copy-done | bytes 65560
  45.5 1.9 %shard_map.48 = f32[2,8,1024]{2,1,0:T(8,128)} custom-call(f32[8,16,128]{2,1,0:T(8,128)} %copy-done, f32[2,15,1024]{2,1,0:T(8,128)} %copy.5.screened_ref), custom_call_target="tpu_custom_call" | custom-call | tf_op jit(solution)/shard_map/pallas_call | solution.py:333
Async XLA Ops:
  5.9 6.5 %collective-permute-start = (f32[4,64,128]{2,1,0:T(8,128)}, f32[4,64,128]{2,1,0:T(8,128)S(1)}, u32[]{:S(2)}, u32[]{:S(2)}) collective-permute-start(f32[4,64,128]{2,1,0:T(8,128)} %get-tuple-element.8), channel_id=1, source_target_pairs={{8,0},{16,8},{24,16},{0,24},{9,1},{17,9},{25,17},{1,25},{10,2},{18... | collective-permute-start | bytes 393224 | tf_op jit(solution)/shard_map/ppermute | solution.py:317
  8.4 7.7 %collective-permute-start.1 = (f32[4,64,128]{2,1,0:T(8,128)}, f32[4,64,128]{2,1,0:T(8,128)S(1)}, u32[]{:S(2)}, u32[]{:S(2)}) collective-permute-start(f32[4,64,128]{2,1,0:T(8,128)} %get-tuple-element.8), channel_id=1, source_target_pairs={{16,0},{24,8},{0,16},{8,24},{17,1},{25,9},{1,17},{9,25},{18,2},{26... | collective-permute-start | bytes 393224 | tf_op jit(solution)/shard_map/ppermute | solution.py:317
  8.9 7.2 %collective-permute-start.2 = (f32[4,64,128]{2,1,0:T(8,128)}, f32[4,64,128]{2,1,0:T(8,128)S(1)}, u32[]{:S(2)}, u32[]{:S(2)}) collective-permute-start(f32[4,64,128]{2,1,0:T(8,128)} %get-tuple-element.8), channel_id=1, source_target_pairs={{24,0},{0,8},{8,16},{16,24},{25,1},{1,9},{9,17},{17,25},{26,2},{2,... | collective-permute-start | bytes 393224 | tf_op jit(solution)/shard_map/ppermute | solution.py:317
  12.5 3.6 %copy-start.1 = (f32[4,64,128]{2,1,0:T(8,128)}, f32[4,64,128]{2,1,0:T(8,128)S(1)}, u32[]{:S(2)}) copy-start(f32[4,64,128]{2,1,0:T(8,128)S(1)} %collective-permute-done.refs_0_) | copy-start | bytes 393220
  16.1 0.6 %copy-start.2 = (f32[4,64,128]{2,1,0:T(8,128)}, f32[4,64,128]{2,1,0:T(8,128)S(1)}, u32[]{:S(2)}) copy-start(f32[4,64,128]{2,1,0:T(8,128)S(1)} %collective-permute-done.1.refs_1_) | copy-start | bytes 393220
  16.1 0.7 %copy-start.3 = (f32[4,64,128]{2,1,0:T(8,128)}, f32[4,64,128]{2,1,0:T(8,128)S(1)}, u32[]{:S(2)}) copy-start(f32[4,64,128]{2,1,0:T(8,128)S(1)} %collective-permute-done.2.refs_2_) | copy-start | bytes 393220
  31.9 6.1 %copy-start.4 = (f32[2,15,1024]{2,0,1:T(2,128)S(1)}, f32[2,15,1024]{2,0,1:T(2,128)}, u32[]{:S(2)}) copy-start(f32[2,15,1024]{2,0,1:T(2,128)} %param.7) | copy-start | bytes 368644
  31.9 13.0 %all-to-all-start = ((f32[8,16,128]{2,1,0:T(8,128)}), f32[8,16,128]{2,1,0:T(8,128)S(1)}, u32[]{:S(2)}, u32[]{:S(2)}) async-start(f32[8,16,128]{2,1,0:T(8,128)} %bitcast.4), calls=%async_computation | async-start | bytes 131072 | tf_op jit(solution)/shard_map/all_to_all | solution.py:331
  44.9 0.6 %copy-start = (f32[8,16,128]{2,1,0:T(8,128)}, f32[8,16,128]{2,1,0:T(8,128)S(1)}, u32[]{:S(2)}) copy-start(f32[8,16,128]{2,1,0:T(8,128)S(1)} %all-to-all-done.green_ref) | copy-start | bytes 196612

commit v2 on v1

v2 whole, which is shorter than its diff:
```python
import functools

import jax
import jax.numpy as jnp
from jax import lax
from jax.experimental import pallas as pl
from jax.experimental.pallas import tpu as pltpu
from jax.sharding import PartitionSpec as P

broadening = 0.25
energy_low = -3.0
energy_high = 3.0

PANEL = 8
SMALL = 2.0**-48


def iota(shape, dim):
    return lax.broadcasted_iota(jnp.int32, shape, dim)


def swap_halves(x):
    return pltpu.roll(x, x.shape[1] // 2, 1)


def low_half(x):
    return iota(x.shape, 1) < x.shape[1] // 2


def sublane_broadcast(x, row):
    return jnp.broadcast_to(x[row : row + 1, :], x.shape)


def complex_times(a, b):
    return a[0] * b[0] - a[1] * b[1], a[0] * b[1] + a[1] * b[0]


def minus(a, b):
    return a[0] - b[0], a[1] - b[1]


def tree_sum(terms):
    while len(terms) > 1:
        paired = [terms[n] + terms[n + 1] for n in range(0, len(terms) - 1, 2)]
        terms = paired + terms[len(paired) * 2 :]
    return terms[0]


def eliminate_panel(real, imag, panel):
    shape = real[0].shape
    half = shape[1] // 2
    lane, sub = iota(shape, 1) & (half - 1), iota(shape, 0)
    inside = (lane // PANEL) == panel
    unit = jnp.where((lane & (PANEL - 1)) == sub, 1.0, 0.0)
    places = [(iota(shape, 1) & half) + (panel * PANEL + c) for c in range(PANEL)]

    def column(x, c):
        return jnp.take_along_axis(x, places[c], axis=1, mode="promise_in_bounds")

    block = [
        (column(real[panel], c) * SMALL, column(imag[panel], c) * SMALL) for c in range(PANEL)
    ]
    rows = (jnp.where(inside, unit, real[panel]), jnp.where(inside, 0.0, imag[panel]))
    scale = (jnp.zeros(shape, jnp.float32), jnp.zeros(shape, jnp.float32))

    def spread(pair, row):
        return sublane_broadcast(pair[0], row), sublane_broadcast(pair[1], row)

    pivot = spread(block[0], 0)
    for step in range(PANEL):
        here = sub == step
        factor = 1.0 / (pivot[0] * pivot[0] + pivot[1] * pivot[1])
        recip = (pivot[0] * factor, -(pivot[1] * factor))
        if step < PANEL - 1:
            product = complex_times(spread(block[step], step + 1), spread(block[step + 1], step))
            pivot = minus(spread(block[step + 1], step + 1), complex_times(product, recip))
        rest = (jnp.where(here, 0.0, block[step][0]), jnp.where(here, 0.0, block[step][1]))
        multiple = complex_times(rest, recip)
        scale = (jnp.where(here, recip[0], scale[0]), jnp.where(here, recip[1], scale[1]))
        for c in range(step + 1, PANEL):
            block[c] = minus(block[c], complex_times(multiple, spread(block[c], step)))
        rows = minus(rows, complex_times(multiple, spread(rows, step)))
    rows = complex_times(rows, (scale[0] * SMALL, scale[1] * SMALL))
    spreads = [spread(rows, c) for c in range(PANEL)]
    others = [(panel + ahead) % len(real) for ahead in range(1, len(real))]
    columns = {group: [] for group in others}
    for c in range(PANEL):
        for group in others:
            columns[group].append((column(real[group], c), column(imag[group], c)))
    new_real, new_imag = list(real), list(imag)
    for group in others:
        terms = [complex_times(a, b) for a, b in zip(columns[group], spreads)]
        new_real[group] = jnp.where(inside, 0.0, real[group]) - tree_sum([t[0] for t in terms])
        new_imag[group] = jnp.where(inside, 0.0, imag[group]) - tree_sum([t[1] for t in terms])
    new_real[panel], new_imag[panel] = rows
    return new_real, new_imag


def invert_pair(first, second):
    low = low_half(first)
    real = jnp.where(low, first, swap_halves(second))
    imag = jnp.where(low, swap_halves(first), second)
    groups = first.shape[0] // PANEL
    real = [real[PANEL * g : PANEL * (g + 1)] for g in range(groups)]
    imag = [imag[PANEL * g : PANEL * (g + 1)] for g in range(groups)]
    for panel in range(groups):
        real, imag = eliminate_panel(real, imag, panel)
    return jnp.concatenate(real, 0), jnp.concatenate(imag, 0)


def side_of_pair(real, imag):
    low = low_half(real)
    return jnp.where(low, real, swap_halves(imag)), jnp.where(low, swap_halves(real), imag)


def times_i(x):
    turned = swap_halves(x)
    return jnp.where(low_half(x), -turned, turned)


def matmul(a, b):
    a_high, b_high = a.astype(jnp.bfloat16), b.astype(jnp.bfloat16)
    a_low = (a - a_high.astype(jnp.float32)).astype(jnp.bfloat16)
    b_low = (b - b_high.astype(jnp.float32)).astype(jnp.bfloat16)
    return jnp.dot(
        jnp.concatenate([a_high, a_high, a_low], 1),
        jnp.concatenate([b_high, b_low, b_high], 0),
        preferred_element_type=jnp.float32,
    )


def pair_solve(real, imag, right_first, right_second):
    low = low_half(real)
    left = jnp.concatenate(
        [
            jnp.concatenate([jnp.where(low, real, 0.0), jnp.where(low, imag, 0.0)], 1),
            jnp.concatenate([jnp.where(low, 0.0, real), jnp.where(low, 0.0, imag)], 1),
        ],
        0,
    )
    rows = real.shape[0]
    firsts, seconds = [], []
    for a, b in zip(right_first, right_second):
        stacked = jnp.concatenate([a, b], 0)
        turned = times_i(stacked)
        right = jnp.concatenate(
            [
                jnp.concatenate([stacked, turned], 1),
                jnp.concatenate([turned, -stacked], 1),
            ],
            0,
        )
        product = matmul(left, right)
        width = stacked.shape[1]
        firsts.append(jnp.concatenate([product[:rows, :width], product[:rows, width:]], 0))
        seconds.append(jnp.concatenate([product[rows:, :width], product[rows:, width:]], 0))
    return jnp.concatenate(firsts, 1), jnp.concatenate(seconds, 1)


def eliminate(block_first, block_second, sides_first, sides_second):
    real, imag = invert_pair(block_first, block_second)
    right_first, right_second = pair_solve(
        real,
        imag,
        [sides_first[1], sides_first[2]],
        [sides_second[1], sides_second[2]],
    )
    results = []
    for sides, right in ((sides_first, right_first), (sides_second, right_second)):
        rows, width = sides[0].shape
        out = matmul(jnp.concatenate([sides[0], sides[3]], 0), right)
        results.append(
            (out[:rows, :width], out[:rows, width:], out[rows:, :width], out[rows:, width:])
        )
    return results


def adjoint(x):
    half = x.shape[1] // 2
    turned = x.T
    return jnp.concatenate([turned[:half], -turned[half:]], 1)


def reduce_kernel(space_count, energy_count, onsite_ref, hopping_ref, sigma_ref, own_ref, reduced_ref):
    orbitals = onsite_ref.shape[-1]
    level = lax.axis_index("energy").astype(jnp.float32)
    energy = energy_low + (energy_high - energy_low) * (level + 0.5) / energy_count
    active = jnp.where(lax.axis_index("space") < space_count - 1, 1.0, 0.0)
    unit = jnp.where(
        iota((orbitals, orbitals), 0) == iota((orbitals, orbitals), 1), 1.0, 0.0
    )
    system = [
        jnp.concatenate(
            [
                energy * unit - onsite_ref[0, n] - sigma_ref[0, n],
                broadening * unit - onsite_ref[1, n] - sigma_ref[1, n],
            ],
            1,
        )
        for n in range(2)
    ]
    within = jnp.concatenate([hopping_ref[0, 0], hopping_ref[1, 0]], 1)
    beyond = jnp.concatenate([hopping_ref[0, 1], hopping_ref[1, 1]], 1) * active
    within_adjoint, beyond_adjoint = adjoint(within), adjoint(beyond)
    own_ref[0], own_ref[1] = system
    own_ref[2], own_ref[3] = within, within_adjoint
    own_ref[4], own_ref[5] = beyond, beyond_adjoint
    sides = (within, within_adjoint, beyond, beyond_adjoint)
    products, unused = eliminate(system[1], system[1], sides, sides)
    reduced_ref[0] = system[0] - products[0]
    reduced_ref[1] = products[3]
    reduced_ref[2] = -products[1]
    reduced_ref[3] = -products[2]


def solve_kernel(count, own_ref, *refs):
    flipped, green_ref = refs[:-1], refs[-1]
    place = lax.axis_index("space")

    def other(turn, part):
        flips = sorted({r ^ ((r + turn) % count) for r in range(count)})
        wanted = place ^ ((place + turn) & (count - 1))
        value = flipped[flips[0] - 1][part]
        for flip in flips[1:]:
            value = jnp.where(wanted == flip, flipped[flip - 1][part], value)
        return value

    even, odd = own_ref[0], own_ref[1]
    within, within_adjoint = own_ref[2], own_ref[3]
    blocks = {turn: other(turn, 0) for turn in range(1, count)}
    for turn in range(1, count - 1):
        blocks[turn + 1] = blocks[turn + 1] - other(turn, 1)
    blocks[0] = odd
    blocks[count] = even - other(count - 1, 1)
    links = {turn: (other(turn, 2), other(turn, 3)) for turn in range(1, count)}
    links[0] = (-own_ref[4], -own_ref[5])
    stride = 1
    while stride < count:
        turns = list(range(stride, count, 2 * stride))
        last = len(turns) == 1
        for start in range(0, len(turns), 2):
            chosen = turns[start : start + 2]
            both = chosen if len(chosen) == 2 else chosen * 2
            sides = [links[t - stride] + links[t] for t in both]
            results = eliminate(blocks[both[0]], blocks[both[1]], sides[0], sides[1])
            for t, (left_left, left_right, right_left, right_right) in zip(chosen, results):
                blocks[t - stride] = blocks[t - stride] - left_left
                blocks[t + stride] = blocks[t + stride] - right_right
                if not last:
                    links[t - stride] = (-left_right, -right_left)
        stride *= 2
    even, odd = blocks[count], blocks[0]
    real, imag = invert_pair(even, odd)
    right_even, right_odd = pair_solve(real, imag, [within], [within_adjoint])
    odd_new = odd - matmul(within_adjoint, right_even)
    even_new = even - matmul(within, right_odd)
    real, imag = invert_pair(even_new, odd_new)
    rows = even.shape[0]
    green_ref[:rows], green_ref[rows:] = side_of_pair(real, imag)


def window_kernel(screened_ref, window_ref, lag_ref):
    sources = window_ref.shape[1]
    lags = screened_ref.shape[1]
    for part in range(2):
        lag_ref[part, : lags - sources] = screened_ref[part, sources:]
        lag_ref[part, lags - sources : lags] = screened_ref[part, :sources]
        for source in range(sources):
            window_ref[part, source] = lag_ref[part, pl.ds(lags - sources - source, sources)]


def convolve_kernel(green_ref, window_ref, out_ref):
    energies, rows, width = green_ref.shape
    low = iota((energies, width), 1) < width // 2
    for tile in range(rows // 2):
        place = pl.ds(tile * width, width)
        first, second = green_ref[:, 2 * tile, :], green_ref[:, 2 * tile + 1, :]
        real = jnp.where(low, first, swap_halves(second))
        imag = jnp.where(low, swap_halves(first), second)
        terms = []
        for source in range(energies):
            green = (
                jnp.broadcast_to(real[source : source + 1], (energies, width)),
                jnp.broadcast_to(imag[source : source + 1], (energies, width)),
            )
            screen = (window_ref[0, source, :, place], window_ref[1, source, :, place])
            terms.append(complex_times(green, screen))
        out_ref[0, :, place] = tree_sum([t[0] for t in terms])
        out_ref[1, :, place] = tree_sum([t[1] for t in terms])


def in_vmem(x):
    return pltpu.with_memory_space_constraint(x, pltpu.VMEM)


def local(onsite, hopping, sigma_prior, screened):
    blocks, orbitals = onsite.shape[1], onsite.shape[-1]
    space_count = lax.axis_size("space")
    energy_count = lax.axis_size("energy")
    if blocks != 2 or sigma_prior.shape[1] != 1 or space_count & (space_count - 1):
        raise ValueError("unsupported placement")
    width = 2 * orbitals
    whole = pl.BlockSpec(memory_space=pltpu.VMEM)
    params = pltpu.CompilerParams(vmem_limit_bytes=24 * 2**20)
    own, reduced = pl.pallas_call(
        functools.partial(reduce_kernel, space_count, energy_count),
        out_shape=(
            pltpu.VMEM((6, orbitals, width), jnp.float32),
            pltpu.VMEM((4, orbitals, width), jnp.float32),
        ),
        compiler_params=params,
        in_specs=[whole] * 3,
        out_specs=(whole, whole),
    )(onsite, hopping, sigma_prior.reshape(onsite.shape))
    held = {0: reduced}
    bit = space_count // 2
    while bit:
        pairs = [(r, r ^ bit) for r in range(space_count)]
        held |= {flip ^ bit: lax.ppermute(held[flip], "space", pairs) for flip in list(held)}
        bit //= 2
    others = [in_vmem(held[flip]) for flip in range(1, space_count)]
    green = pl.pallas_call(
        functools.partial(solve_kernel, space_count),
        out_shape=pltpu.VMEM((blocks * orbitals, width), jnp.float32),
        compiler_params=params,
        in_specs=[whole] * space_count,
        out_specs=whole,
    )(in_vmem(own), *others)
    pieces = green.reshape(energy_count, blocks * orbitals // energy_count, width)
    gathered = lax.all_to_all(pieces, "energy", split_axis=0, concat_axis=0, tiled=True)
    lag_count, entries = screened.shape[1:]
    window = pl.pallas_call(
        window_kernel,
        out_shape=pltpu.VMEM((2, energy_count, energy_count, entries), jnp.float32),
        compiler_params=params,
        in_specs=[whole],
        out_specs=whole,
        scratch_shapes=[pltpu.VMEM((2, lag_count + 1, entries), jnp.float32)],
        cost_estimate=pl.CostEstimate(
            flops=0, transcendentals=0, bytes_accessed=16 * energy_count**2 * entries
        ),
    )(screened)
    return pl.pallas_call(
        convolve_kernel,
        out_shape=jax.ShapeDtypeStruct((2, energy_count, entries), jnp.float32),
        compiler_params=params,
        in_specs=[whole, whole],
        out_specs=whole,
    )(in_vmem(gathered), in_vmem(window))


def solution(mesh):
    in_specs = (
        P(None, "space", None, None),
        P(None, "space", None, None),
        P(None, "energy", "space", None, None),
        P(None, None, ("space", "energy")),
    )
    out_specs = P(None, None, ("space", "energy"))
    return jax.shard_map(local, mesh=mesh, in_specs=in_specs, out_specs=out_specs, check_vma=False)
```

time: 47.6 us -> 37.7 us (0.79)
  Pallas kernels: 22.3 us -> 13.8 us
  waiting for transfers between devices: 13.2 us -> 11.6 us
  local copies, waits for them, and re-layouts: 2.01 us -> 2.76 us
  other arithmetic: 0.62 us -> 0 us
    pallas_call x2 -> x3, Pallas kernels: 20.4 us -> 13 us  [the longest x1 10.1 us: local(): pl.pallas_call(functools.partial(solve_kernel, space_count), out_shape=pl...]
    ppermute x3, waiting for transfers between devices: 6.96 us -> 4.84 us  [local(): lax.ppermute(held[flip], 'space', pairs)]
    pallas_call x1, Pallas kernels: 1.89 us -> 0.79 us  [local(): pl.pallas_call(convolve_kernel, out_shape=jax.ShapeDtypeStruct((2, energy...]
    unnamed x11 -> x9, local copies, waits for them, and re-layouts: 2.01 us -> 2.76 us
    another operation x1 -> x0, other arithmetic: 0.62 us -> none  [local(): jnp.stack([energy, active])]
    all_to_all x1, waiting for transfers between devices: 6.21 us -> 6.75 us  [local(): lax.all_to_all(pieces, 'energy', split_axis=0, concat_axis=0, tiled=True)]
  transfers between devices with their start and end apart: 4 -> 4, of which waited for: 3 -> 3; matrix products, arithmetic and copies ran while one was open for 1% -> 0% of each run, Pallas kernels for 0% -> 0%
where the time goes in v2:
time: 37.7 us; the launch traced here: 37.4 us
  Pallas kernels  13.8 us (37%)
  waiting for transfers between devices  11.6 us (31%)
  starting transfers between devices  9.22 us (24%)
  local copies, waits for them, and re-layouts  2.76 us (7%)
    pallas_call x1, Pallas kernels, local(): pl.pallas_call(functools.partial(solve_kernel, space_count), out_shape=pl...  10.1 us
    all_to_all x1, waiting for transfers between devices, local(): lax.all_to_all(pieces, 'energy', split_axis=0, concat_axis=0, tiled=True)  6.75 us
    all_to_all x1, starting transfers between devices, local(): lax.all_to_all(pieces, 'energy', split_axis=0, concat_axis=0, tiled=True)  6.15 us
    ppermute x3, waiting for transfers between devices, local(): lax.ppermute(held[flip], 'space', pairs)  4.84 us
    ppermute x3, starting transfers between devices, local(): lax.ppermute(held[flip], 'space', pairs)  3.07 us
    pallas_call x1, Pallas kernels, local(): pl.pallas_call(functools.partial(reduce_kernel, space_count, energy_count...  2.87 us
    unnamed x9, local copies, waits for them, and re-layouts  2.76 us
    pallas_call x1, Pallas kernels, local(): pl.pallas_call(convolve_kernel, out_shape=jax.ShapeDtypeStruct((2, energy...  0.79 us
  transfers between devices with their start and end apart: 4, of which 3 were waited for; matrix products, arithmetic and copies ran while one was open for 0% of the time, Pallas kernels for 0%

profile of v2, /device:TPU:0, one launch (start us, length us, event | category | flops | bytes accessed | tf_op | source)
XLA Modules:
  0.0 37.4 jit_solution(13716336991093840731)
XLA Ops:
  0.0 0.0 copy-start
  0.0 0.9 %copy-done = f32[2,2,64,64]{3,2,1,0:T(8,128)S(1)} copy-done((f32[2,2,64,64]{3,2,1,0:T(8,128)S(1)}, f32[2,2,64,64]{3,2,1,0:T(8,128)}, u32[]{:S(2)}) %copy-start) | copy-done | bytes 65560
  0.9 0.0 copy-start.1
  0.9 0.9 %copy-done.1 = f32[2,2,64,64]{3,2,1,0:T(8,128)S(1)} copy-done((f32[2,2,64,64]{3,2,1,0:T(8,128)S(1)}, f32[2,2,64,64]{3,2,1,0:T(8,128)}, u32[]{:S(2)}) %copy-start.1) | copy-done | bytes 65560
  1.8 0.0 copy-start.2
  1.8 0.9 %copy-done.2 = f32[2,1,2,64,64]{4,3,2,1,0:T(8,128)S(1)} copy-done((f32[2,1,2,64,64]{4,3,2,1,0:T(8,128)S(1)}, f32[2,1,2,64,64]{4,3,2,1,0:T(8,128)}, u32[]{:S(2)}) %copy-start.2) | copy-done | bytes 65560
  2.7 2.9 %shard_map.46 = (f32[6,64,128]{2,1,0:T(8,128)S(1)}, f32[4,64,128]{2,1,0:T(8,128)S(1)}) custom-call(f32[2,2,64,64]{3,2,1,0:T(8,128)S(1)} %copy-done, f32[2,2,64,64]{3,2,1,0:T(8,128)S(1)} %copy-done.1, f32[2,2,64,64]{3,2,1,0:T(8,128)S(1)} %bitcast.2), custom_call_target="tpu_custom_call" | custom-call | tf_op jit(solution)/shard_map/pallas_call | solution.py:305
  5.6 3.1 %collective-permute-start.1 = (f32[4,64,128]{2,1,0:T(8,128)S(1)}, f32[4,64,128]{2,1,0:T(8,128)S(1)}, u32[]{:S(2)}, u32[]{:S(2)}) collective-permute-start(f32[4,64,128]{2,1,0:T(8,128)S(1)} %get-tuple-element.8), channel_id=1, source_target_pairs={{0,16},{8,24},{16,0},{24,8},{1,17},{9,25},{17,1},{25,9},{2,18},{10... | collective-permute-start | bytes 393224 | tf_op jit(solution)/shard_map/ppermute | solution.py:319
  8.7 0.0 collective-permute-start
  8.7 3.5 %collective-permute-done.1.refs_1_ = f32[4,64,128]{2,1,0:T(8,128)S(1)} collective-permute-done((f32[4,64,128]{2,1,0:T(8,128)S(1)}, f32[4,64,128]{2,1,0:T(8,128)S(1)}, u32[]{:S(2)}, u32[]{:S(2)}) %collective-permute-start.1) | collective-permute-done | bytes 131104 | tf_op jit(solution)/shard_map/ppermute | solution.py:319
  12.2 0.0 collective-permute-start.2
  12.2 0.0 collective-permute-done.refs_0_
  12.2 1.3 %collective-permute-done.2.refs_2_ = f32[4,64,128]{2,1,0:T(8,128)S(1)} collective-permute-done((f32[4,64,128]{2,1,0:T(8,128)S(1)}, f32[4,64,128]{2,1,0:T(8,128)S(1)}, u32[]{:S(2)}, u32[]{:S(2)}) %collective-permute-start.2) | collective-permute-done | bytes 131104 | tf_op jit(solution)/shard_map/ppermute | solution.py:319
  13.5 10.1 %shard_map.47 = f32[128,128]{1,0:T(8,128)} custom-call(f32[6,64,128]{2,1,0:T(8,128)S(1)} %get-tuple-element.7.own_ref, f32[4,64,128]{2,1,0:T(8,128)S(1)} %collective-permute-done.refs_0_, f32[4,64,128]{2,1,0:T(8,128)S(1)} %collective-permute-done.1.refs_1_, f32[4,64,128]{2,1,0:T(8,128)S(1)} %collective-permute-done.2.refs_2_), custom_call_target="tpu_custom_call" | custom-call | tf_op jit(solution)/shard_map/pallas_call | solution.py:322
  23.6 0.0 copy-start.3
  23.6 6.1 %all-to-all-start = ((f32[8,16,128]{2,1,0:T(8,128)}), f32[8,16,128]{2,1,0:T(8,128)S(1)}, u32[]{:S(2)}, u32[]{:S(2)}) async-start(f32[8,16,128]{2,1,0:T(8,128)} %bitcast.1), calls=%async_computation | async-start | bytes 131072 | tf_op jit(solution)/shard_map/all_to_all | solution.py:330
  29.7 0.0 copy-done.3
  29.8 0.1 shard_map.48.window_ref
  29.9 6.7 %all-to-all-done.green_ref = f32[8,16,128]{2,1,0:T(8,128)S(1)} async-done(((f32[8,16,128]{2,1,0:T(8,128)}), f32[8,16,128]{2,1,0:T(8,128)S(1)}, u32[]{:S(2)}, u32[]{:S(2)}) %all-to-all-start) | async-done | bytes 65568 | tf_op jit(solution)/shard_map/all_to_all | solution.py:330
  36.6 0.8 %shard_map.49 = f32[2,8,1024]{2,1,0:T(8,128)} custom-call(f32[8,16,128]{2,1,0:T(8,128)S(1)} %all-to-all-done.green_ref, f32[2,8,8,1024]{3,2,1,0:T(8,128)S(1)} %shard_map.48.window_ref), custom_call_target="tpu_custom_call" | custom-call | tf_op jit(solution)/shard_map/pallas_call | solution.py:343
  (1 shorter events, 0.0 us)
Async XLA Ops:
  0.0 0.9 %copy-start = (f32[2,2,64,64]{3,2,1,0:T(8,128)S(1)}, f32[2,2,64,64]{3,2,1,0:T(8,128)}, u32[]{:S(2)}) copy-start(f32[2,2,64,64]{3,2,1,0:T(8,128)} %onsite_ref.1) | copy-start | bytes 196612
  0.9 0.9 %copy-start.1 = (f32[2,2,64,64]{3,2,1,0:T(8,128)S(1)}, f32[2,2,64,64]{3,2,1,0:T(8,128)}, u32[]{:S(2)}) copy-start(f32[2,2,64,64]{3,2,1,0:T(8,128)} %hopping_ref.1) | copy-start | bytes 196612
  1.8 0.9 %copy-start.2 = (f32[2,1,2,64,64]{4,3,2,1,0:T(8,128)S(1)}, f32[2,1,2,64,64]{4,3,2,1,0:T(8,128)}, u32[]{:S(2)}) copy-start(f32[2,1,2,64,64]{4,3,2,1,0:T(8,128)} %param.6) | copy-start | bytes 196612
  5.6 6.6 %collective-permute-start.1 = (f32[4,64,128]{2,1,0:T(8,128)S(1)}, f32[4,64,128]{2,1,0:T(8,128)S(1)}, u32[]{:S(2)}, u32[]{:S(2)}) collective-permute-start(f32[4,64,128]{2,1,0:T(8,128)S(1)} %get-tuple-element.8), channel_id=1, source_target_pairs={{0,16},{8,24},{16,0},{24,8},{1,17},{9,25},{17,1},{25,9},{2,18},{10... | collective-permute-start | bytes 393224 | tf_op jit(solution)/shard_map/ppermute | solution.py:319
  8.7 3.5 %collective-permute-start = (f32[4,64,128]{2,1,0:T(8,128)S(1)}, f32[4,64,128]{2,1,0:T(8,128)S(1)}, u32[]{:S(2)}, u32[]{:S(2)}) collective-permute-start(f32[4,64,128]{2,1,0:T(8,128)S(1)} %get-tuple-element.8), channel_id=1, source_target_pairs={{0,8},{8,0},{16,24},{24,16},{1,9},{9,1},{17,25},{25,17},{2,10},{10... | collective-permute-start | bytes 393224 | tf_op jit(solution)/shard_map/ppermute | solution.py:319
  12.2 1.3 %collective-permute-start.2 = (f32[4,64,128]{2,1,0:T(8,128)S(1)}, f32[4,64,128]{2,1,0:T(8,128)S(1)}, u32[]{:S(2)}, u32[]{:S(2)}) collective-permute-start(f32[4,64,128]{2,1,0:T(8,128)S(1)} %collective-permute-done.1.refs_1_), channel_id=1, source_target_pairs={{0,8},{8,0},{16,24},{24,16},{1,9},{9,1},{17,25},{25,17},{2,10},{10... | collective-permute-start | bytes 393224 | tf_op jit(solution)/shard_map/ppermute | solution.py:319
  23.6 6.2 %copy-start.3 = (f32[2,15,1024]{2,0,1:T(2,128)S(1)}, f32[2,15,1024]{2,0,1:T(2,128)}, u32[]{:S(2)}) copy-start(f32[2,15,1024]{2,0,1:T(2,128)} %param.7) | copy-start | bytes 368644
  23.6 13.1 %all-to-all-start = ((f32[8,16,128]{2,1,0:T(8,128)}), f32[8,16,128]{2,1,0:T(8,128)S(1)}, u32[]{:S(2)}, u32[]{:S(2)}) async-start(f32[8,16,128]{2,1,0:T(8,128)} %bitcast.1), calls=%async_computation | async-start | bytes 131072 | tf_op jit(solution)/shard_map/all_to_all | solution.py:330

commit v3 on v2

--- a/solution.py
+++ b/solution.py
@@ -46,54 +46,65 @@
     return terms[0]
 
 
-def eliminate_panel(real, imag, panel):
-    shape = real[0].shape
+def invert_groups(real, imag):
+    real, imag = list(real), list(imag)
+    count, shape = len(real), real[0].shape
     half = shape[1] // 2
     lane, sub = iota(shape, 1) & (half - 1), iota(shape, 0)
-    inside = (lane // PANEL) == panel
     unit = jnp.where((lane & (PANEL - 1)) == sub, 1.0, 0.0)
-    places = [(iota(shape, 1) & half) + (panel * PANEL + c) for c in range(PANEL)]
-
-    def column(x, c):
-        return jnp.take_along_axis(x, places[c], axis=1, mode="promise_in_bounds")
-
-    block = [
-        (column(real[panel], c) * SMALL, column(imag[panel], c) * SMALL) for c in range(PANEL)
-    ]
-    rows = (jnp.where(inside, unit, real[panel]), jnp.where(inside, 0.0, imag[panel]))
-    scale = (jnp.zeros(shape, jnp.float32), jnp.zeros(shape, jnp.float32))
+
+    def columns(panel, groups):
+        found = {group: [] for group in groups}
+        for c in range(PANEL):
+            place = (iota(shape, 1) & half) + (panel * PANEL + c)
+            for group in groups:
+                found[group].append(
+                    tuple(
+                        jnp.take_along_axis(x, place, axis=1, mode="promise_in_bounds")
+                        for x in (real[group], imag[group])
+                    )
+                )
+        return found
 
     def spread(pair, row):
         return sublane_broadcast(pair[0], row), sublane_broadcast(pair[1], row)
 
-    pivot = spread(block[0], 0)
-    for step in range(PANEL):
-        here = sub == step
-        factor = 1.0 / (pivot[0] * pivot[0] + pivot[1] * pivot[1])
-        recip = (pivot[0] * factor, -(pivot[1] * factor))
-        if step < PANEL - 1:
-            product = complex_times(spread(block[step], step + 1), spread(block[step + 1], step))
-            pivot = minus(spread(block[step + 1], step + 1), complex_times(product, recip))
-        rest = (jnp.where(here, 0.0, block[step][0]), jnp.where(here, 0.0, block[step][1]))
-        multiple = complex_times(rest, recip)
-        scale = (jnp.where(here, recip[0], scale[0]), jnp.where(here, recip[1], scale[1]))
-        for c in range(step + 1, PANEL):
-            block[c] = minus(block[c], complex_times(multiple, spread(block[c], step)))
-        rows = minus(rows, complex_times(multiple, spread(rows, step)))
-    rows = complex_times(rows, (scale[0] * SMALL, scale[1] * SMALL))
-    spreads = [spread(rows, c) for c in range(PANEL)]
-    others = [(panel + ahead) % len(real) for ahead in range(1, len(real))]
-    columns = {group: [] for group in others}
-    for c in range(PANEL):
-        for group in others:
-            columns[group].append((column(real[group], c), column(imag[group], c)))
-    new_real, new_imag = list(real), list(imag)
-    for group in others:
-        terms = [complex_times(a, b) for a, b in zip(columns[group], spreads)]
-        new_real[group] = jnp.where(inside, 0.0, real[group]) - tree_sum([t[0] for t in terms])
-        new_imag[group] = jnp.where(inside, 0.0, imag[group]) - tree_sum([t[1] for t in terms])
-    new_real[panel], new_imag[panel] = rows
-    return new_real, new_imag
+    block = columns(0, [0])[0]
+    for panel in range(count):
+        following = (panel + 1) % count
+        rest = [group for group in range(count) if group not in (panel, following)]
+        inside = (lane // PANEL) == panel
+        column = columns(panel, [following])
+        column |= columns(panel, rest)
+        block = [(a * SMALL, b * SMALL) for a, b in block]
+        rows = (jnp.where(inside, unit, real[panel]), jnp.where(inside, 0.0, imag[panel]))
+        scale = (jnp.zeros(shape, jnp.float32), jnp.zeros(shape, jnp.float32))
+        pivot = spread(block[0], 0)
+        for step in range(PANEL):
+            here = sub == step
+            factor = 1.0 / (pivot[0] * pivot[0] + pivot[1] * pivot[1])
+            recip = (pivot[0] * factor, -(pivot[1] * factor))
+            if step < PANEL - 1:
+                product = complex_times(
+                    spread(block[step], step + 1), spread(block[step + 1], step)
+                )
+                pivot = minus(spread(block[step + 1], step + 1), complex_times(product, recip))
+            outer = (jnp.where(here, 0.0, block[step][0]), jnp.where(here, 0.0, block[step][1]))
+            multiple = complex_times(outer, recip)
+            scale = (jnp.where(here, recip[0], scale[0]), jnp.where(here, recip[1], scale[1]))
+            for c in range(step + 1, PANEL):
+                block[c] = minus(block[c], complex_times(multiple, spread(block[c], step)))
+            rows = minus(rows, complex_times(multiple, spread(rows, step)))
+        rows = complex_times(rows, (scale[0] * SMALL, scale[1] * SMALL))
+        spreads = [spread(rows, c) for c in range(PANEL)]
+        real[panel], imag[panel] = rows
+        for group in [following] + rest:
+            terms = [complex_times(a, b) for a, b in zip(column[group], spreads)]
+            real[group] = jnp.where(inside, 0.0, real[group]) - tree_sum([t[0] for t in terms])
+            imag[group] = jnp.where(inside, 0.0, imag[group]) - tree_sum([t[1] for t in terms])
+            if group == following and panel < count - 1:
+                block = columns(following, [following])[following]
+    return real, imag
 
 
 def invert_pair(first, second):
@@ -103,8 +114,7 @@
     groups = first.shape[0] // PANEL
     real = [real[PANEL * g : PANEL * (g + 1)] for g in range(groups)]
     imag = [imag[PANEL * g : PANEL * (g + 1)] for g in range(groups)]
-    for panel in range(groups):
-        real, imag = eliminate_panel(real, imag, panel)
+    real, imag = invert_groups(real, imag)
     return jnp.concatenate(real, 0), jnp.concatenate(imag, 0)
 
 
@@ -214,7 +224,7 @@
 
 
 def solve_kernel(count, own_ref, *refs):
-    flipped, green_ref = refs[:-1], refs[-1]
+    flipped, (keep_ref, give_ref, green_ref) = refs[:-3], refs[-3:]
     place = lax.axis_index("space")
 
     def other(turn, part):
@@ -255,8 +265,15 @@
     odd_new = odd - matmul(within_adjoint, right_even)
     even_new = even - matmul(within, right_odd)
     real, imag = invert_pair(even_new, odd_new)
-    rows = even.shape[0]
-    green_ref[:rows], green_ref[rows:] = side_of_pair(real, imag)
+    pieces, rows = green_ref.shape[:2]
+    first, second = side_of_pair(real, imag)
+    for piece in range(pieces // 2):
+        green_ref[piece] = first[piece * rows : (piece + 1) * rows]
+        green_ref[pieces // 2 + piece] = second[piece * rows : (piece + 1) * rows]
+    rank = lax.axis_index("energy")
+    for slot in range(pieces // 2):
+        keep_ref[slot] = green_ref[rank ^ (2 * slot)]
+        give_ref[slot] = green_ref[rank ^ (2 * slot + 1)]
 
 
 def window_kernel(screened_ref, window_ref, lag_ref):
@@ -269,22 +286,35 @@
             window_ref[part, source] = lag_ref[part, pl.ds(lags - sources - source, sources)]
 
 
-def convolve_kernel(green_ref, window_ref, out_ref):
-    energies, rows, width = green_ref.shape
-    low = iota((energies, width), 1) < width // 2
+def exchange_kernel(dests, kept_ref, got_ref, keep_ref, give_ref):
+    held = kept_ref.shape[0]
+    for source in range(2 * held // dests):
+        ref, base = (kept_ref, 0) if source * dests < held else (got_ref, held)
+        for dest in range(dests):
+            to_ref = give_ref if dest % 2 else keep_ref
+            to_ref[(source * dests + dest) // 2] = ref[source * dests + dest - base]
+
+
+def convolve_kernel(kept_ref, got_ref, window_ref, out_ref):
+    half, rows, width = kept_ref.shape
+    energies = 2 * half
+    low = iota((half, width), 1) < width // 2
+    rank = lax.axis_index("energy")
     for tile in range(rows // 2):
         place = pl.ds(tile * width, width)
-        first, second = green_ref[:, 2 * tile, :], green_ref[:, 2 * tile + 1, :]
-        real = jnp.where(low, first, swap_halves(second))
-        imag = jnp.where(low, swap_halves(first), second)
         terms = []
-        for source in range(energies):
-            green = (
-                jnp.broadcast_to(real[source : source + 1], (energies, width)),
-                jnp.broadcast_to(imag[source : source + 1], (energies, width)),
-            )
-            screen = (window_ref[0, source, :, place], window_ref[1, source, :, place])
-            terms.append(complex_times(green, screen))
+        for part, ref in enumerate((kept_ref, got_ref)):
+            first, second = ref[:, 2 * tile, :], ref[:, 2 * tile + 1, :]
+            real = jnp.where(low, first, swap_halves(second))
+            imag = jnp.where(low, swap_halves(first), second)
+            for n in range(half):
+                source = rank ^ (part * half + n)
+                green = (
+                    jnp.broadcast_to(real[n : n + 1], (energies, width)),
+                    jnp.broadcast_to(imag[n : n + 1], (energies, width)),
+                )
+                screen = (window_ref[0, source, :, place], window_ref[1, source, :, place])
+                terms.append(complex_times(green, screen))
         out_ref[0, :, place] = tree_sum([t[0] for t in terms])
         out_ref[1, :, place] = tree_sum([t[1] for t in terms])
 
@@ -308,7 +338,6 @@
             pltpu.VMEM((6, orbitals, width), jnp.float32),
             pltpu.VMEM((4, orbitals, width), jnp.float32),
         ),
-        compiler_params=params,
         in_specs=[whole] * 3,
         out_specs=(whole, whole),
     )(onsite, hopping, sigma_prior.reshape(onsite.shape))
@@ -319,15 +348,30 @@
         held |= {flip ^ bit: lax.ppermute(held[flip], "space", pairs) for flip in list(held)}
         bit //= 2
     others = [in_vmem(held[flip]) for flip in range(1, space_count)]
-    green = pl.pallas_call(
+    piece = (blocks * orbitals // energy_count, width)
+    halves = (pltpu.VMEM((energy_count // 2,) + piece, jnp.float32),) * 2
+    keep, give = pl.pallas_call(
         functools.partial(solve_kernel, space_count),
-        out_shape=pltpu.VMEM((blocks * orbitals, width), jnp.float32),
+        out_shape=halves,
         compiler_params=params,
         in_specs=[whole] * space_count,
-        out_specs=whole,
+        out_specs=(whole, whole),
+        scratch_shapes=[pltpu.VMEM((energy_count,) + piece, jnp.float32)],
     )(in_vmem(own), *others)
-    pieces = green.reshape(energy_count, blocks * orbitals // energy_count, width)
-    gathered = lax.all_to_all(pieces, "energy", split_axis=0, concat_axis=0, tiled=True)
+    bit = 1
+    while True:
+        pairs = [(r, r ^ bit) for r in range(energy_count)]
+        got = lax.ppermute(give, "energy", pairs)
+        bit *= 2
+        if bit == energy_count:
+            break
+        keep, give = pl.pallas_call(
+            functools.partial(exchange_kernel, energy_count // bit),
+            out_shape=halves,
+            compiler_params=params,
+            in_specs=[whole, whole],
+            out_specs=(whole, whole),
+        )(in_vmem(keep), in_vmem(got))
     lag_count, entries = screened.shape[1:]
     window = pl.pallas_call(
         window_kernel,
@@ -344,9 +388,9 @@
         convolve_kernel,
         out_shape=jax.ShapeDtypeStruct((2, energy_count, entries), jnp.float32),
         compiler_params=params,
-        in_specs=[whole, whole],
+        in_specs=[whole, whole, whole],
         out_specs=whole,
-    )(in_vmem(gathered), in_vmem(window))
+    )(in_vmem(keep), in_vmem(got), in_vmem(window))
 
 
 def solution(mesh):

time: 37.7 us -> 35 us (0.928)
  local copies, waits for them, and re-layouts: 2.76 us -> 0.05 us
  waiting for transfers between devices: 11.6 us -> 11 us
  Pallas kernels: 13.8 us -> 14.3 us
    all_to_all x1 -> x0, waiting for transfers between devices: 6.75 us -> none  [local(): lax.all_to_all(pieces, 'energy', split_axis=0, concat_axis=0, tiled=True)]
    ppermute x0 -> x3, starting transfers between devices: none -> 6.38 us  [local(): got = lax.ppermute(give, 'energy', pairs)]
    ppermute x0 -> x3, waiting for transfers between devices: none -> 6.18 us  [local(): got = lax.ppermute(give, 'energy', pairs)]
    all_to_all x1 -> x0, starting transfers between devices: 6.15 us -> none  [local(): lax.all_to_all(pieces, 'energy', split_axis=0, concat_axis=0, tiled=True)]
    unnamed x9 -> x3, local copies, waits for them, and re-layouts: 2.76 us -> 0.05 us
    pallas_call x1, Pallas kernels: 2.87 us -> 3.89 us  [local(): pl.pallas_call(functools.partial(reduce_kernel, space_count, energy_count...]
    pallas_call x1 -> x3, Pallas kernels: 10.1 us -> 9.51 us  [the longest x1 9.5 us: local(): pl.pallas_call(functools.partial(solve_kernel, space_count), out_shape=ha...]
  transfers between devices with their start and end apart: 4 -> 6, of which waited for: 3 -> 5; matrix products, arithmetic and copies ran while one was open for 0% -> 0% of each run, Pallas kernels for 0% -> 0%
where the time goes in v3:
time: 35 us; the launch traced here: 34.8 us
  Pallas kernels  14.3 us (41%)
  waiting for transfers between devices  11 us (31%)
  starting transfers between devices  9.43 us (27%)
    pallas_call x1, Pallas kernels, local(): pl.pallas_call(functools.partial(solve_kernel, space_count), out_shape=ha...  9.5 us
    ppermute x3, starting transfers between devices, local(): got = lax.ppermute(give, 'energy', pairs)  6.38 us
    ppermute x3, waiting for transfers between devices, local(): got = lax.ppermute(give, 'energy', pairs)  6.18 us
    ppermute x3, waiting for transfers between devices, local(): lax.ppermute(held[flip], 'space', pairs)  4.84 us
    pallas_call x1, Pallas kernels, local(): pl.pallas_call(functools.partial(reduce_kernel, space_count, energy_count...  3.89 us
    ppermute x3, starting transfers between devices, local(): lax.ppermute(held[flip], 'space', pairs)  3.05 us
    pallas_call x1, Pallas kernels, local(): pl.pallas_call(convolve_kernel, out_shape=jax.ShapeDtypeStruct((2, energy...  0.79 us
  transfers between devices with their start and end apart: 6, of which 5 were waited for; matrix products, arithmetic and copies ran while one was open for 0% of the time, Pallas kernels for 0%

profile of v3, /device:TPU:0, one launch (start us, length us, event | category | flops | bytes accessed | tf_op | source)
XLA Modules:
  0.0 34.8 jit_solution(6103682076847707607)
XLA Ops:
  0.0 3.9 %shard_map.46 = (f32[6,64,128]{2,1,0:T(8,128)S(1)}, f32[4,64,128]{2,1,0:T(8,128)S(1)}) custom-call(f32[2,2,64,64]{3,2,1,0:T(8,128)} %onsite_ref.1, f32[2,2,64,64]{3,2,1,0:T(8,128)} %hopping_ref.1, f32[2,2,64,64]{3,2,1,0:T(8,128)} %bitcast.1), custom_call_target="tpu_custom_call" | custom-call | tf_op jit(solution)/shard_map/pallas_call | solution.py:335
  3.9 3.0 %collective-permute-start.1 = (f32[4,64,128]{2,1,0:T(8,128)S(1)}, f32[4,64,128]{2,1,0:T(8,128)S(1)}, u32[]{:S(2)}, u32[]{:S(2)}) collective-permute-start(f32[4,64,128]{2,1,0:T(8,128)S(1)} %get-tuple-element.14), channel_id=1, source_target_pairs={{0,16},{8,24},{16,0},{24,8},{1,17},{9,25},{17,1},{25,9},{2,18},{10... | collective-permute-start | bytes 393224 | tf_op jit(solution)/shard_map/ppermute | solution.py:348
  6.9 0.0 collective-permute-start
  7.0 3.5 %collective-permute-done.1.refs_1_ = f32[4,64,128]{2,1,0:T(8,128)S(1)} collective-permute-done((f32[4,64,128]{2,1,0:T(8,128)S(1)}, f32[4,64,128]{2,1,0:T(8,128)S(1)}, u32[]{:S(2)}, u32[]{:S(2)}) %collective-permute-start.1) | collective-permute-done | bytes 131104 | tf_op jit(solution)/shard_map/ppermute | solution.py:348
  10.4 0.0 collective-permute-start.2
  10.4 0.0 collective-permute-done.refs_0_
  10.5 1.3 %collective-permute-done.2.refs_2_ = f32[4,64,128]{2,1,0:T(8,128)S(1)} collective-permute-done((f32[4,64,128]{2,1,0:T(8,128)S(1)}, f32[4,64,128]{2,1,0:T(8,128)S(1)}, u32[]{:S(2)}, u32[]{:S(2)}) %collective-permute-start.2) | collective-permute-done | bytes 131104 | tf_op jit(solution)/shard_map/ppermute | solution.py:348
  11.8 9.5 %shard_map.47 = (f32[4,16,128]{2,1,0:T(8,128)S(1)}, f32[4,16,128]{2,1,0:T(8,128)S(1)}) custom-call(f32[6,64,128]{2,1,0:T(8,128)S(1)} %get-tuple-element.13.own_ref, f32[4,64,128]{2,1,0:T(8,128)S(1)} %collective-permute-done.refs_0_, f32[4,64,128]{2,1,0:T(8,128)S(1)} %collective-permute-done.1.refs_1_, f32[4,64,128]{2,1,0:T(8,128)S(1)} %collective-permute-done.2.refs_2_), custom_call_target="tpu_custom_call" | custom-call | tf_op jit(solution)/shard_map/pallas_call | solution.py:353
  21.3 0.0 copy-start
  21.3 1.8 %collective-permute-start.3 = (f32[4,16,128]{2,1,0:T(8,128)S(1)}, f32[4,16,128]{2,1,0:T(8,128)S(1)}, u32[]{:S(2)}, u32[]{:S(2)}) collective-permute-start(f32[4,16,128]{2,1,0:T(8,128)S(1)} %get-tuple-element.16), channel_id=1, source_target_pairs={{0,1},{1,0},{2,3},{3,2},{4,5},{5,4},{6,7},{7,6},{8,9},{9,8},{10,11... | collective-permute-start | bytes 98312 | tf_op jit(solution)/shard_map/ppermute | solution.py:364
  23.1 2.2 %collective-permute-done.3.got_ref = f32[4,16,128]{2,1,0:T(8,128)S(1)} collective-permute-done((f32[4,16,128]{2,1,0:T(8,128)S(1)}, f32[4,16,128]{2,1,0:T(8,128)S(1)}, u32[]{:S(2)}, u32[]{:S(2)}) %collective-permute-start.3) | collective-permute-done | bytes 32800 | tf_op jit(solution)/shard_map/ppermute | solution.py:364
  25.3 1.8 %collective-permute-start.4 = (f32[4,16,128]{2,1,0:T(8,128)S(1)}, f32[4,16,128]{2,1,0:T(8,128)S(1)}, u32[]{:S(2)}, u32[]{:S(2)}) collective-permute-start(f32[4,16,128]{2,1,0:T(8,128)S(1)} %get-tuple-element.18), channel_id=1, source_target_pairs={{0,2},{1,3},{2,0},{3,1},{4,6},{5,7},{6,4},{7,5},{8,10},{9,11},{10,... | collective-permute-start | bytes 98312 | tf_op jit(solution)/shard_map/ppermute | solution.py:364
  27.1 2.1 %collective-permute-done.4.got_ref = f32[4,16,128]{2,1,0:T(8,128)S(1)} collective-permute-done((f32[4,16,128]{2,1,0:T(8,128)S(1)}, f32[4,16,128]{2,1,0:T(8,128)S(1)}, u32[]{:S(2)}, u32[]{:S(2)}) %collective-permute-start.4) | collective-permute-done | bytes 32800 | tf_op jit(solution)/shard_map/ppermute | solution.py:364
  29.2 2.8 %collective-permute-start.5 = (f32[4,16,128]{2,1,0:T(8,128)S(1)}, f32[4,16,128]{2,1,0:T(8,128)S(1)}, u32[]{:S(2)}, u32[]{:S(2)}) collective-permute-start(f32[4,16,128]{2,1,0:T(8,128)S(1)} %get-tuple-element.20), channel_id=1, source_target_pairs={{0,4},{1,5},{2,6},{3,7},{4,0},{5,1},{6,2},{7,3},{8,12},{9,13},{10,... | collective-permute-start | bytes 98312 | tf_op jit(solution)/shard_map/ppermute | solution.py:364
  32.0 0.0 copy-done
  32.1 0.1 shard_map.50.window_ref
  32.2 1.9 %collective-permute-done.5.got_ref = f32[4,16,128]{2,1,0:T(8,128)S(1)} collective-permute-done((f32[4,16,128]{2,1,0:T(8,128)S(1)}, f32[4,16,128]{2,1,0:T(8,128)S(1)}, u32[]{:S(2)}, u32[]{:S(2)}) %collective-permute-start.5) | collective-permute-done | bytes 32800 | tf_op jit(solution)/shard_map/ppermute | solution.py:364
  34.0 0.8 %shard_map.51 = f32[2,8,1024]{2,1,0:T(8,128)} custom-call(f32[4,16,128]{2,1,0:T(8,128)S(1)} %get-tuple-element.19.kept_ref, f32[4,16,128]{2,1,0:T(8,128)S(1)} %collective-permute-done.5.got_ref, f32[2,8,8,1024]{3,2,1,0:T(8,128)S(1)} %shard_map.50.window_ref), custom_call_target="tpu_custom_call" | custom-call | tf_op jit(solution)/shard_map/pallas_call | solution.py:387
  (3 shorter events, 0.1 us)
Async XLA Ops:
  3.9 6.5 %collective-permute-start.1 = (f32[4,64,128]{2,1,0:T(8,128)S(1)}, f32[4,64,128]{2,1,0:T(8,128)S(1)}, u32[]{:S(2)}, u32[]{:S(2)}) collective-permute-start(f32[4,64,128]{2,1,0:T(8,128)S(1)} %get-tuple-element.14), channel_id=1, source_target_pairs={{0,16},{8,24},{16,0},{24,8},{1,17},{9,25},{17,1},{25,9},{2,18},{10... | collective-permute-start | bytes 393224 | tf_op jit(solution)/shard_map/ppermute | solution.py:348
  6.9 3.5 %collective-permute-start = (f32[4,64,128]{2,1,0:T(8,128)S(1)}, f32[4,64,128]{2,1,0:T(8,128)S(1)}, u32[]{:S(2)}, u32[]{:S(2)}) collective-permute-start(f32[4,64,128]{2,1,0:T(8,128)S(1)} %get-tuple-element.14), channel_id=1, source_target_pairs={{0,8},{8,0},{16,24},{24,16},{1,9},{9,1},{17,25},{25,17},{2,10},{10... | collective-permute-start | bytes 393224 | tf_op jit(solution)/shard_map/ppermute | solution.py:348
  10.4 1.3 %collective-permute-start.2 = (f32[4,64,128]{2,1,0:T(8,128)S(1)}, f32[4,64,128]{2,1,0:T(8,128)S(1)}, u32[]{:S(2)}, u32[]{:S(2)}) collective-permute-start(f32[4,64,128]{2,1,0:T(8,128)S(1)} %collective-permute-done.1.refs_1_), channel_id=1, source_target_pairs={{0,8},{8,0},{16,24},{24,16},{1,9},{9,1},{17,25},{25,17},{2,10},{10... | collective-permute-start | bytes 393224 | tf_op jit(solution)/shard_map/ppermute | solution.py:348
  21.3 10.7 %copy-start = (f32[2,15,1024]{2,0,1:T(2,128)S(1)}, f32[2,15,1024]{2,0,1:T(2,128)}, u32[]{:S(2)}) copy-start(f32[2,15,1024]{2,0,1:T(2,128)} %param.7) | copy-start | bytes 368644
  21.3 4.0 %collective-permute-start.3 = (f32[4,16,128]{2,1,0:T(8,128)S(1)}, f32[4,16,128]{2,1,0:T(8,128)S(1)}, u32[]{:S(2)}, u32[]{:S(2)}) collective-permute-start(f32[4,16,128]{2,1,0:T(8,128)S(1)} %get-tuple-element.16), channel_id=1, source_target_pairs={{0,1},{1,0},{2,3},{3,2},{4,5},{5,4},{6,7},{7,6},{8,9},{9,8},{10,11... | collective-permute-start | bytes 98312 | tf_op jit(solution)/shard_map/ppermute | solution.py:364
  25.3 3.9 %collective-permute-start.4 = (f32[4,16,128]{2,1,0:T(8,128)S(1)}, f32[4,16,128]{2,1,0:T(8,128)S(1)}, u32[]{:S(2)}, u32[]{:S(2)}) collective-permute-start(f32[4,16,128]{2,1,0:T(8,128)S(1)} %get-tuple-element.18), channel_id=1, source_target_pairs={{0,2},{1,3},{2,0},{3,1},{4,6},{5,7},{6,4},{7,5},{8,10},{9,11},{10,... | collective-permute-start | bytes 98312 | tf_op jit(solution)/shard_map/ppermute | solution.py:364
  29.2 4.8 %collective-permute-start.5 = (f32[4,16,128]{2,1,0:T(8,128)S(1)}, f32[4,16,128]{2,1,0:T(8,128)S(1)}, u32[]{:S(2)}, u32[]{:S(2)}) collective-permute-start(f32[4,16,128]{2,1,0:T(8,128)S(1)} %get-tuple-element.20), channel_id=1, source_target_pairs={{0,4},{1,5},{2,6},{3,7},{4,0},{5,1},{6,2},{7,3},{8,12},{9,13},{10,... | collective-permute-start | bytes 98312 | tf_op jit(solution)/shard_map/ppermute | solution.py:364

commit v4 on v3

--- a/solution.py
+++ b/solution.py
@@ -46,21 +46,25 @@
     return terms[0]
 
 
-def invert_groups(real, imag):
+def invert_groups(real, imag, paired):
     real, imag = list(real), list(imag)
     count, shape = len(real), real[0].shape
     half = shape[1] // 2
-    lane, sub = iota(shape, 1) & (half - 1), iota(shape, 0)
+    lane, sub = iota(shape, 1), iota(shape, 0)
+    if paired:
+        lane = lane & (half - 1)
     unit = jnp.where((lane & (PANEL - 1)) == sub, 1.0, 0.0)
 
     def columns(panel, groups):
         found = {group: [] for group in groups}
-        for c in range(PANEL):
-            place = (iota(shape, 1) & half) + (panel * PANEL + c)
+        for c in range(panel * PANEL, panel * PANEL + PANEL):
+            place = (iota(shape, 1) & half) + c
             for group in groups:
                 found[group].append(
                     tuple(
                         jnp.take_along_axis(x, place, axis=1, mode="promise_in_bounds")
+                        if paired
+                        else jnp.broadcast_to(x[:, c : c + 1], shape)
                         for x in (real[group], imag[group])
                     )
                 )
@@ -107,14 +111,14 @@
     return real, imag
 
 
-def invert_pair(first, second):
+def invert_pair(first, second, paired=True):
     low = low_half(first)
     real = jnp.where(low, first, swap_halves(second))
     imag = jnp.where(low, swap_halves(first), second)
     groups = first.shape[0] // PANEL
     real = [real[PANEL * g : PANEL * (g + 1)] for g in range(groups)]
     imag = [imag[PANEL * g : PANEL * (g + 1)] for g in range(groups)]
-    real, imag = invert_groups(real, imag)
+    real, imag = invert_groups(real, imag, paired)
     return jnp.concatenate(real, 0), jnp.concatenate(imag, 0)
 
 
@@ -185,6 +189,28 @@
     return results
 
 
+def eliminate_one(block, sides):
+    real, imag = invert_pair(block, sides[1], False)
+    inverse, from_left = side_of_pair(real, imag)
+    turned = times_i(sides[2])
+    rows, width = block.shape
+    from_right = matmul(
+        inverse,
+        jnp.concatenate(
+            [jnp.concatenate([sides[2], turned], 1), jnp.concatenate([turned, -sides[2]], 1)], 0
+        ),
+    )
+    right = jnp.concatenate(
+        [
+            jnp.concatenate([from_left, times_i(from_left)], 0),
+            jnp.concatenate([from_right[:, :width], from_right[:, width:]], 0),
+        ],
+        1,
+    )
+    out = matmul(jnp.concatenate([sides[0], sides[3]], 0), right)
+    return out[:rows, :width], out[:rows, width:], out[rows:, :width], out[rows:, width:]
+
+
 def adjoint(x):
     half = x.shape[1] // 2
     turned = x.T
@@ -216,7 +242,7 @@
     own_ref[2], own_ref[3] = within, within_adjoint
     own_ref[4], own_ref[5] = beyond, beyond_adjoint
     sides = (within, within_adjoint, beyond, beyond_adjoint)
-    products, unused = eliminate(system[1], system[1], sides, sides)
+    products = eliminate_one(system[1], sides)
     reduced_ref[0] = system[0] - products[0]
     reduced_ref[1] = products[3]
     reduced_ref[2] = -products[1]
@@ -250,9 +276,11 @@
         last = len(turns) == 1
         for start in range(0, len(turns), 2):
             chosen = turns[start : start + 2]
-            both = chosen if len(chosen) == 2 else chosen * 2
-            sides = [links[t - stride] + links[t] for t in both]
-            results = eliminate(blocks[both[0]], blocks[both[1]], sides[0], sides[1])
+            sides = [links[t - stride] + links[t] for t in chosen]
+            if len(chosen) == 1:
+                results = [eliminate_one(blocks[chosen[0]], sides[0])]
+            else:
+                results = eliminate(blocks[chosen[0]], blocks[chosen[1]], sides[0], sides[1])
             for t, (left_left, left_right, right_left, right_right) in zip(chosen, results):
                 blocks[t - stride] = blocks[t - stride] - left_left
                 blocks[t + stride] = blocks[t + stride] - right_right

time: 35 us -> 34.4 us (0.983)
  Pallas kernels: 14.3 us -> 13.7 us
    pallas_call x1, Pallas kernels: 3.89 us -> 3.52 us  [local(): pl.pallas_call(functools.partial(reduce_kernel, space_count, energy_count...]
where the time goes in v4:
time: 34.4 us; the launch traced here: 34.2 us
  Pallas kernels  13.7 us (40%)
  waiting for transfers between devices  11 us (32%)
  starting transfers between devices  9.45 us (27%)
    pallas_call x1, Pallas kernels, local(): pl.pallas_call(functools.partial(solve_kernel, space_count), out_shape=ha...  9.29 us
    ppermute x3, starting transfers between devices, local(): got = lax.ppermute(give, 'energy', pairs)  6.39 us
    ppermute x3, waiting for transfers between devices, local(): got = lax.ppermute(give, 'energy', pairs)  6.17 us
    ppermute x3, waiting for transfers between devices, local(): lax.ppermute(held[flip], 'space', pairs)  4.84 us
    pallas_call x1, Pallas kernels, local(): pl.pallas_call(functools.partial(reduce_kernel, space_count, energy_count...  3.52 us
    ppermute x3, starting transfers between devices, local(): lax.ppermute(held[flip], 'space', pairs)  3.07 us
    pallas_call x1, Pallas kernels, local(): pl.pallas_call(convolve_kernel, out_shape=jax.ShapeDtypeStruct((2, energy...  0.79 us
  transfers between devices with their start and end apart: 6, of which 5 were waited for; matrix products, arithmetic and copies ran while one was open for 0% of the time, Pallas kernels for 0%

profile of v4, /device:TPU:0, one launch (start us, length us, event | category | flops | bytes accessed | tf_op | source)
XLA Modules:
  0.0 34.2 jit_solution(14601052574788923925)
XLA Ops:
  0.0 3.5 %shard_map.46 = (f32[6,64,128]{2,1,0:T(8,128)S(1)}, f32[4,64,128]{2,1,0:T(8,128)S(1)}) custom-call(f32[2,2,64,64]{3,2,1,0:T(8,128)} %onsite_ref.1, f32[2,2,64,64]{3,2,1,0:T(8,128)} %hopping_ref.1, f32[2,2,64,64]{3,2,1,0:T(8,128)} %bitcast.1), custom_call_target="tpu_custom_call" | custom-call | tf_op jit(solution)/shard_map/pallas_call | solution.py:363
  3.5 3.1 %collective-permute-start.1 = (f32[4,64,128]{2,1,0:T(8,128)S(1)}, f32[4,64,128]{2,1,0:T(8,128)S(1)}, u32[]{:S(2)}, u32[]{:S(2)}) collective-permute-start(f32[4,64,128]{2,1,0:T(8,128)S(1)} %get-tuple-element.14), channel_id=1, source_target_pairs={{0,16},{8,24},{16,0},{24,8},{1,17},{9,25},{17,1},{25,9},{2,18},{10... | collective-permute-start | bytes 393224 | tf_op jit(solution)/shard_map/ppermute | solution.py:376
  6.6 0.0 collective-permute-start
  6.6 3.5 %collective-permute-done.1.refs_1_ = f32[4,64,128]{2,1,0:T(8,128)S(1)} collective-permute-done((f32[4,64,128]{2,1,0:T(8,128)S(1)}, f32[4,64,128]{2,1,0:T(8,128)S(1)}, u32[]{:S(2)}, u32[]{:S(2)}) %collective-permute-start.1) | collective-permute-done | bytes 131104 | tf_op jit(solution)/shard_map/ppermute | solution.py:376
  10.1 0.0 collective-permute-start.2
  10.1 0.0 collective-permute-done.refs_0_
  10.1 1.3 %collective-permute-done.2.refs_2_ = f32[4,64,128]{2,1,0:T(8,128)S(1)} collective-permute-done((f32[4,64,128]{2,1,0:T(8,128)S(1)}, f32[4,64,128]{2,1,0:T(8,128)S(1)}, u32[]{:S(2)}, u32[]{:S(2)}) %collective-permute-start.2) | collective-permute-done | bytes 131104 | tf_op jit(solution)/shard_map/ppermute | solution.py:376
  11.4 9.3 %shard_map.47 = (f32[4,16,128]{2,1,0:T(8,128)S(1)}, f32[4,16,128]{2,1,0:T(8,128)S(1)}) custom-call(f32[6,64,128]{2,1,0:T(8,128)S(1)} %get-tuple-element.13.own_ref, f32[4,64,128]{2,1,0:T(8,128)S(1)} %collective-permute-done.refs_0_, f32[4,64,128]{2,1,0:T(8,128)S(1)} %collective-permute-done.1.refs_1_, f32[4,64,128]{2,1,0:T(8,128)S(1)} %collective-permute-done.2.refs_2_), custom_call_target="tpu_custom_call" | custom-call | tf_op jit(solution)/shard_map/pallas_call | solution.py:381
  20.7 0.0 copy-start
  20.7 1.8 %collective-permute-start.3 = (f32[4,16,128]{2,1,0:T(8,128)S(1)}, f32[4,16,128]{2,1,0:T(8,128)S(1)}, u32[]{:S(2)}, u32[]{:S(2)}) collective-permute-start(f32[4,16,128]{2,1,0:T(8,128)S(1)} %get-tuple-element.16), channel_id=1, source_target_pairs={{0,1},{1,0},{2,3},{3,2},{4,5},{5,4},{6,7},{7,6},{8,9},{9,8},{10,11... | collective-permute-start | bytes 98312 | tf_op jit(solution)/shard_map/ppermute | solution.py:392
  22.5 2.2 %collective-permute-done.3.got_ref = f32[4,16,128]{2,1,0:T(8,128)S(1)} collective-permute-done((f32[4,16,128]{2,1,0:T(8,128)S(1)}, f32[4,16,128]{2,1,0:T(8,128)S(1)}, u32[]{:S(2)}, u32[]{:S(2)}) %collective-permute-start.3) | collective-permute-done | bytes 32800 | tf_op jit(solution)/shard_map/ppermute | solution.py:392
  24.7 1.8 %collective-permute-start.4 = (f32[4,16,128]{2,1,0:T(8,128)S(1)}, f32[4,16,128]{2,1,0:T(8,128)S(1)}, u32[]{:S(2)}, u32[]{:S(2)}) collective-permute-start(f32[4,16,128]{2,1,0:T(8,128)S(1)} %get-tuple-element.18), channel_id=1, source_target_pairs={{0,2},{1,3},{2,0},{3,1},{4,6},{5,7},{6,4},{7,5},{8,10},{9,11},{10,... | collective-permute-start | bytes 98312 | tf_op jit(solution)/shard_map/ppermute | solution.py:392
  26.5 2.1 %collective-permute-done.4.got_ref = f32[4,16,128]{2,1,0:T(8,128)S(1)} collective-permute-done((f32[4,16,128]{2,1,0:T(8,128)S(1)}, f32[4,16,128]{2,1,0:T(8,128)S(1)}, u32[]{:S(2)}, u32[]{:S(2)}) %collective-permute-start.4) | collective-permute-done | bytes 32800 | tf_op jit(solution)/shard_map/ppermute | solution.py:392
  28.6 2.8 %collective-permute-start.5 = (f32[4,16,128]{2,1,0:T(8,128)S(1)}, f32[4,16,128]{2,1,0:T(8,128)S(1)}, u32[]{:S(2)}, u32[]{:S(2)}) collective-permute-start(f32[4,16,128]{2,1,0:T(8,128)S(1)} %get-tuple-element.20), channel_id=1, source_target_pairs={{0,4},{1,5},{2,6},{3,7},{4,0},{5,1},{6,2},{7,3},{8,12},{9,13},{10,... | collective-permute-start | bytes 98312 | tf_op jit(solution)/shard_map/ppermute | solution.py:392
  31.5 0.0 copy-done
  31.5 0.1 shard_map.50.window_ref
  31.6 1.9 %collective-permute-done.5.got_ref = f32[4,16,128]{2,1,0:T(8,128)S(1)} collective-permute-done((f32[4,16,128]{2,1,0:T(8,128)S(1)}, f32[4,16,128]{2,1,0:T(8,128)S(1)}, u32[]{:S(2)}, u32[]{:S(2)}) %collective-permute-start.5) | collective-permute-done | bytes 32800 | tf_op jit(solution)/shard_map/ppermute | solution.py:392
  33.5 0.8 %shard_map.51 = f32[2,8,1024]{2,1,0:T(8,128)} custom-call(f32[4,16,128]{2,1,0:T(8,128)S(1)} %get-tuple-element.19.kept_ref, f32[4,16,128]{2,1,0:T(8,128)S(1)} %collective-permute-done.5.got_ref, f32[2,8,8,1024]{3,2,1,0:T(8,128)S(1)} %shard_map.50.window_ref), custom_call_target="tpu_custom_call" | custom-call | tf_op jit(solution)/shard_map/pallas_call | solution.py:415
  (3 shorter events, 0.1 us)
Async XLA Ops:
  3.5 6.6 %collective-permute-start.1 = (f32[4,64,128]{2,1,0:T(8,128)S(1)}, f32[4,64,128]{2,1,0:T(8,128)S(1)}, u32[]{:S(2)}, u32[]{:S(2)}) collective-permute-start(f32[4,64,128]{2,1,0:T(8,128)S(1)} %get-tuple-element.14), channel_id=1, source_target_pairs={{0,16},{8,24},{16,0},{24,8},{1,17},{9,25},{17,1},{25,9},{2,18},{10... | collective-permute-start | bytes 393224 | tf_op jit(solution)/shard_map/ppermute | solution.py:376
  6.6 3.5 %collective-permute-start = (f32[4,64,128]{2,1,0:T(8,128)S(1)}, f32[4,64,128]{2,1,0:T(8,128)S(1)}, u32[]{:S(2)}, u32[]{:S(2)}) collective-permute-start(f32[4,64,128]{2,1,0:T(8,128)S(1)} %get-tuple-element.14), channel_id=1, source_target_pairs={{0,8},{8,0},{16,24},{24,16},{1,9},{9,1},{17,25},{25,17},{2,10},{10... | collective-permute-start | bytes 393224 | tf_op jit(solution)/shard_map/ppermute | solution.py:376
  10.1 1.3 %collective-permute-start.2 = (f32[4,64,128]{2,1,0:T(8,128)S(1)}, f32[4,64,128]{2,1,0:T(8,128)S(1)}, u32[]{:S(2)}, u32[]{:S(2)}) collective-permute-start(f32[4,64,128]{2,1,0:T(8,128)S(1)} %collective-permute-done.1.refs_1_), channel_id=1, source_target_pairs={{0,8},{8,0},{16,24},{24,16},{1,9},{9,1},{17,25},{25,17},{2,10},{10... | collective-permute-start | bytes 393224 | tf_op jit(solution)/shard_map/ppermute | solution.py:376
  20.7 10.7 %copy-start = (f32[2,15,1024]{2,0,1:T(2,128)S(1)}, f32[2,15,1024]{2,0,1:T(2,128)}, u32[]{:S(2)}) copy-start(f32[2,15,1024]{2,0,1:T(2,128)} %param.7) | copy-start | bytes 368644
  20.7 4.0 %collective-permute-start.3 = (f32[4,16,128]{2,1,0:T(8,128)S(1)}, f32[4,16,128]{2,1,0:T(8,128)S(1)}, u32[]{:S(2)}, u32[]{:S(2)}) collective-permute-start(f32[4,16,128]{2,1,0:T(8,128)S(1)} %get-tuple-element.16), channel_id=1, source_target_pairs={{0,1},{1,0},{2,3},{3,2},{4,5},{5,4},{6,7},{7,6},{8,9},{9,8},{10,11... | collective-permute-start | bytes 98312 | tf_op jit(solution)/shard_map/ppermute | solution.py:392
  24.7 3.9 %collective-permute-start.4 = (f32[4,16,128]{2,1,0:T(8,128)S(1)}, f32[4,16,128]{2,1,0:T(8,128)S(1)}, u32[]{:S(2)}, u32[]{:S(2)}) collective-permute-start(f32[4,16,128]{2,1,0:T(8,128)S(1)} %get-tuple-element.18), channel_id=1, source_target_pairs={{0,2},{1,3},{2,0},{3,1},{4,6},{5,7},{6,4},{7,5},{8,10},{9,11},{10,... | collective-permute-start | bytes 98312 | tf_op jit(solution)/shard_map/ppermute | solution.py:392
  28.6 4.8 %collective-permute-start.5 = (f32[4,16,128]{2,1,0:T(8,128)S(1)}, f32[4,16,128]{2,1,0:T(8,128)S(1)}, u32[]{:S(2)}, u32[]{:S(2)}) collective-permute-start(f32[4,16,128]{2,1,0:T(8,128)S(1)} %get-tuple-element.20), channel_id=1, source_target_pairs={{0,4},{1,5},{2,6},{3,7},{4,0},{5,1},{6,2},{7,3},{8,12},{9,13},{10,... | collective-permute-start | bytes 98312 | tf_op jit(solution)/shard_map/ppermute | solution.py:392

commit v5 on v4

--- a/solution.py
+++ b/solution.py
@@ -288,13 +288,21 @@
                     links[t - stride] = (-left_right, -right_left)
         stride *= 2
     even, odd = blocks[count], blocks[0]
-    real, imag = invert_pair(even, odd)
-    right_even, right_odd = pair_solve(real, imag, [within], [within_adjoint])
-    odd_new = odd - matmul(within_adjoint, right_even)
-    even_new = even - matmul(within, right_odd)
-    real, imag = invert_pair(even_new, odd_new)
+    inverse, from_odd = side_of_pair(*invert_pair(odd, within_adjoint, False))
+    both = matmul(
+        within,
+        jnp.concatenate(
+            [
+                jnp.concatenate([from_odd, inverse], 1),
+                jnp.concatenate([times_i(from_odd), times_i(inverse)], 1),
+            ],
+            0,
+        ),
+    )
+    width = even.shape[1]
+    first, onward = side_of_pair(*invert_pair(even - both[:, :width], both[:, width:], False))
+    second = inverse + matmul(from_odd, jnp.concatenate([onward, times_i(onward)], 0))
     pieces, rows = green_ref.shape[:2]
-    first, second = side_of_pair(real, imag)
     for piece in range(pieces // 2):
         green_ref[piece] = first[piece * rows : (piece + 1) * rows]
         green_ref[pieces // 2 + piece] = second[piece * rows : (piece + 1) * rows]

time: 34.4 us -> 34 us (0.988)
  Pallas kernels: 13.7 us -> 13.3 us
    pallas_call x1, Pallas kernels: 9.29 us -> 8.92 us  [local(): pl.pallas_call(functools.partial(solve_kernel, space_count), out_shape=ha...]
where the time goes in v5:
time: 34 us; the launch traced here: 33.9 us
  Pallas kernels  13.3 us (39%)
  waiting for transfers between devices  11 us (32%)
  starting transfers between devices  9.45 us (28%)
    pallas_call x1, Pallas kernels, local(): pl.pallas_call(functools.partial(solve_kernel, space_count), out_shape=ha...  8.92 us
    ppermute x3, starting transfers between devices, local(): got = lax.ppermute(give, 'energy', pairs)  6.38 us
    ppermute x3, waiting for transfers between devices, local(): got = lax.ppermute(give, 'energy', pairs)  6.18 us
    ppermute x3, waiting for transfers between devices, local(): lax.ppermute(held[flip], 'space', pairs)  4.84 us
    pallas_call x1, Pallas kernels, local(): pl.pallas_call(functools.partial(reduce_kernel, space_count, energy_count...  3.52 us
    ppermute x3, starting transfers between devices, local(): lax.ppermute(held[flip], 'space', pairs)  3.07 us
    pallas_call x1, Pallas kernels, local(): pl.pallas_call(convolve_kernel, out_shape=jax.ShapeDtypeStruct((2, energy...  0.79 us
  transfers between devices with their start and end apart: 6, of which 5 were waited for; matrix products, arithmetic and copies ran while one was open for 0% of the time, Pallas kernels for 0%

profile of v5, /device:TPU:0, one launch (start us, length us, event | category | flops | bytes accessed | tf_op | source)
XLA Modules:
  0.0 33.9 jit_solution(2810990886161038290)
XLA Ops:
  0.0 3.5 %shard_map.46 = (f32[6,64,128]{2,1,0:T(8,128)S(1)}, f32[4,64,128]{2,1,0:T(8,128)S(1)}) custom-call(f32[2,2,64,64]{3,2,1,0:T(8,128)} %onsite_ref.1, f32[2,2,64,64]{3,2,1,0:T(8,128)} %hopping_ref.1, f32[2,2,64,64]{3,2,1,0:T(8,128)} %bitcast.1), custom_call_target="tpu_custom_call" | custom-call | tf_op jit(solution)/shard_map/pallas_call | solution.py:371
  3.5 3.1 %collective-permute-start.1 = (f32[4,64,128]{2,1,0:T(8,128)S(1)}, f32[4,64,128]{2,1,0:T(8,128)S(1)}, u32[]{:S(2)}, u32[]{:S(2)}) collective-permute-start(f32[4,64,128]{2,1,0:T(8,128)S(1)} %get-tuple-element.14), channel_id=1, source_target_pairs={{0,16},{8,24},{16,0},{24,8},{1,17},{9,25},{17,1},{25,9},{2,18},{10... | collective-permute-start | bytes 393224 | tf_op jit(solution)/shard_map/ppermute | solution.py:384
  6.6 0.0 collective-permute-start
  6.6 3.5 %collective-permute-done.1.refs_1_ = f32[4,64,128]{2,1,0:T(8,128)S(1)} collective-permute-done((f32[4,64,128]{2,1,0:T(8,128)S(1)}, f32[4,64,128]{2,1,0:T(8,128)S(1)}, u32[]{:S(2)}, u32[]{:S(2)}) %collective-permute-start.1) | collective-permute-done | bytes 131104 | tf_op jit(solution)/shard_map/ppermute | solution.py:384
  10.1 0.0 collective-permute-start.2
  10.1 0.0 collective-permute-done.refs_0_
  10.1 1.3 %collective-permute-done.2.refs_2_ = f32[4,64,128]{2,1,0:T(8,128)S(1)} collective-permute-done((f32[4,64,128]{2,1,0:T(8,128)S(1)}, f32[4,64,128]{2,1,0:T(8,128)S(1)}, u32[]{:S(2)}, u32[]{:S(2)}) %collective-permute-start.2) | collective-permute-done | bytes 131104 | tf_op jit(solution)/shard_map/ppermute | solution.py:384
  11.4 8.9 %shard_map.47 = (f32[4,16,128]{2,1,0:T(8,128)S(1)}, f32[4,16,128]{2,1,0:T(8,128)S(1)}) custom-call(f32[6,64,128]{2,1,0:T(8,128)S(1)} %get-tuple-element.13.own_ref, f32[4,64,128]{2,1,0:T(8,128)S(1)} %collective-permute-done.refs_0_, f32[4,64,128]{2,1,0:T(8,128)S(1)} %collective-permute-done.1.refs_1_, f32[4,64,128]{2,1,0:T(8,128)S(1)} %collective-permute-done.2.refs_2_), custom_call_target="tpu_custom_call" | custom-call | tf_op jit(solution)/shard_map/pallas_call | solution.py:389
  20.4 0.0 copy-start
  20.4 1.8 %collective-permute-start.3 = (f32[4,16,128]{2,1,0:T(8,128)S(1)}, f32[4,16,128]{2,1,0:T(8,128)S(1)}, u32[]{:S(2)}, u32[]{:S(2)}) collective-permute-start(f32[4,16,128]{2,1,0:T(8,128)S(1)} %get-tuple-element.16), channel_id=1, source_target_pairs={{0,1},{1,0},{2,3},{3,2},{4,5},{5,4},{6,7},{7,6},{8,9},{9,8},{10,11... | collective-permute-start | bytes 98312 | tf_op jit(solution)/shard_map/ppermute | solution.py:400
  22.1 2.2 %collective-permute-done.3.got_ref = f32[4,16,128]{2,1,0:T(8,128)S(1)} collective-permute-done((f32[4,16,128]{2,1,0:T(8,128)S(1)}, f32[4,16,128]{2,1,0:T(8,128)S(1)}, u32[]{:S(2)}, u32[]{:S(2)}) %collective-permute-start.3) | collective-permute-done | bytes 32800 | tf_op jit(solution)/shard_map/ppermute | solution.py:400
  24.4 1.8 %collective-permute-start.4 = (f32[4,16,128]{2,1,0:T(8,128)S(1)}, f32[4,16,128]{2,1,0:T(8,128)S(1)}, u32[]{:S(2)}, u32[]{:S(2)}) collective-permute-start(f32[4,16,128]{2,1,0:T(8,128)S(1)} %get-tuple-element.18), channel_id=1, source_target_pairs={{0,2},{1,3},{2,0},{3,1},{4,6},{5,7},{6,4},{7,5},{8,10},{9,11},{10,... | collective-permute-start | bytes 98312 | tf_op jit(solution)/shard_map/ppermute | solution.py:400
  26.2 2.1 %collective-permute-done.4.got_ref = f32[4,16,128]{2,1,0:T(8,128)S(1)} collective-permute-done((f32[4,16,128]{2,1,0:T(8,128)S(1)}, f32[4,16,128]{2,1,0:T(8,128)S(1)}, u32[]{:S(2)}, u32[]{:S(2)}) %collective-permute-start.4) | collective-permute-done | bytes 32800 | tf_op jit(solution)/shard_map/ppermute | solution.py:400
  28.3 2.8 %collective-permute-start.5 = (f32[4,16,128]{2,1,0:T(8,128)S(1)}, f32[4,16,128]{2,1,0:T(8,128)S(1)}, u32[]{:S(2)}, u32[]{:S(2)}) collective-permute-start(f32[4,16,128]{2,1,0:T(8,128)S(1)} %get-tuple-element.20), channel_id=1, source_target_pairs={{0,4},{1,5},{2,6},{3,7},{4,0},{5,1},{6,2},{7,3},{8,12},{9,13},{10,... | collective-permute-start | bytes 98312 | tf_op jit(solution)/shard_map/ppermute | solution.py:400
  31.1 0.0 copy-done
  31.1 0.1 shard_map.50.window_ref
  31.2 1.9 %collective-permute-done.5.got_ref = f32[4,16,128]{2,1,0:T(8,128)S(1)} collective-permute-done((f32[4,16,128]{2,1,0:T(8,128)S(1)}, f32[4,16,128]{2,1,0:T(8,128)S(1)}, u32[]{:S(2)}, u32[]{:S(2)}) %collective-permute-start.5) | collective-permute-done | bytes 32800 | tf_op jit(solution)/shard_map/ppermute | solution.py:400
  33.1 0.8 %shard_map.51 = f32[2,8,1024]{2,1,0:T(8,128)} custom-call(f32[4,16,128]{2,1,0:T(8,128)S(1)} %get-tuple-element.19.kept_ref, f32[4,16,128]{2,1,0:T(8,128)S(1)} %collective-permute-done.5.got_ref, f32[2,8,8,1024]{3,2,1,0:T(8,128)S(1)} %shard_map.50.window_ref), custom_call_target="tpu_custom_call" | custom-call | tf_op jit(solution)/shard_map/pallas_call | solution.py:423
  (3 shorter events, 0.1 us)
Async XLA Ops:
  3.5 6.6 %collective-permute-start.1 = (f32[4,64,128]{2,1,0:T(8,128)S(1)}, f32[4,64,128]{2,1,0:T(8,128)S(1)}, u32[]{:S(2)}, u32[]{:S(2)}) collective-permute-start(f32[4,64,128]{2,1,0:T(8,128)S(1)} %get-tuple-element.14), channel_id=1, source_target_pairs={{0,16},{8,24},{16,0},{24,8},{1,17},{9,25},{17,1},{25,9},{2,18},{10... | collective-permute-start | bytes 393224 | tf_op jit(solution)/shard_map/ppermute | solution.py:384
  6.6 3.5 %collective-permute-start = (f32[4,64,128]{2,1,0:T(8,128)S(1)}, f32[4,64,128]{2,1,0:T(8,128)S(1)}, u32[]{:S(2)}, u32[]{:S(2)}) collective-permute-start(f32[4,64,128]{2,1,0:T(8,128)S(1)} %get-tuple-element.14), channel_id=1, source_target_pairs={{0,8},{8,0},{16,24},{24,16},{1,9},{9,1},{17,25},{25,17},{2,10},{10... | collective-permute-start | bytes 393224 | tf_op jit(solution)/shard_map/ppermute | solution.py:384
  10.1 1.3 %collective-permute-start.2 = (f32[4,64,128]{2,1,0:T(8,128)S(1)}, f32[4,64,128]{2,1,0:T(8,128)S(1)}, u32[]{:S(2)}, u32[]{:S(2)}) collective-permute-start(f32[4,64,128]{2,1,0:T(8,128)S(1)} %collective-permute-done.1.refs_1_), channel_id=1, source_target_pairs={{0,8},{8,0},{16,24},{24,16},{1,9},{9,1},{17,25},{25,17},{2,10},{10... | collective-permute-start | bytes 393224 | tf_op jit(solution)/shard_map/ppermute | solution.py:384
  20.4 10.7 %copy-start = (f32[2,15,1024]{2,0,1:T(2,128)S(1)}, f32[2,15,1024]{2,0,1:T(2,128)}, u32[]{:S(2)}) copy-start(f32[2,15,1024]{2,0,1:T(2,128)} %param.7) | copy-start | bytes 368644
  20.4 4.0 %collective-permute-start.3 = (f32[4,16,128]{2,1,0:T(8,128)S(1)}, f32[4,16,128]{2,1,0:T(8,128)S(1)}, u32[]{:S(2)}, u32[]{:S(2)}) collective-permute-start(f32[4,16,128]{2,1,0:T(8,128)S(1)} %get-tuple-element.16), channel_id=1, source_target_pairs={{0,1},{1,0},{2,3},{3,2},{4,5},{5,4},{6,7},{7,6},{8,9},{9,8},{10,11... | collective-permute-start | bytes 98312 | tf_op jit(solution)/shard_map/ppermute | solution.py:400
  24.4 3.9 %collective-permute-start.4 = (f32[4,16,128]{2,1,0:T(8,128)S(1)}, f32[4,16,128]{2,1,0:T(8,128)S(1)}, u32[]{:S(2)}, u32[]{:S(2)}) collective-permute-start(f32[4,16,128]{2,1,0:T(8,128)S(1)} %get-tuple-element.18), channel_id=1, source_target_pairs={{0,2},{1,3},{2,0},{3,1},{4,6},{5,7},{6,4},{7,5},{8,10},{9,11},{10,... | collective-permute-start | bytes 98312 | tf_op jit(solution)/shard_map/ppermute | solution.py:400
  28.3 4.8 %collective-permute-start.5 = (f32[4,16,128]{2,1,0:T(8,128)S(1)}, f32[4,16,128]{2,1,0:T(8,128)S(1)}, u32[]{:S(2)}, u32[]{:S(2)}) collective-permute-start(f32[4,16,128]{2,1,0:T(8,128)S(1)} %get-tuple-element.20), channel_id=1, source_target_pairs={{0,4},{1,5},{2,6},{3,7},{4,0},{5,1},{6,2},{7,3},{8,12},{9,13},{10,... | collective-permute-start | bytes 98312 | tf_op jit(solution)/shard_map/ppermute | solution.py:400
